TPU v7x, 32 devices: a whole 2x2x4 slice. The times are simulated.
32 devices in a mesh: dp: 16 (over z, x, core), tp: 2 (over y).
Axes of the slice: x: 2, y: 2, z: 4, core: 2. Of those that a mesh axis runs over, the one named last changes fastest.
Arguments:
- tokens: bfloat16 [3072, 3584], P('dp', 'tp'), may hold values from -6 to 6
- cotangent: bfloat16 [3072, 3584], P('dp', 'tp'), may hold values from -6 to 6
- working: bfloat16 [16, 2, 3, 2048, 3584], P('dp', 'tp'), may hold values from -0.09375 to 0.09375
- degraded: int32 [16], P('dp'), may hold values from 0 to 1, as said below
- block_map: int32 [16, 16], P('dp'), may hold values from 0 to 1, as said below
- master: float32 [3, 2048, 3584], P(None, ('tp', 'dp')), may hold values from -6 to 6
- moment_one: float32 [3, 2048, 3584], P(None, ('tp', 'dp')), may hold values from -6 to 6
- moment_two: float32 [3, 2048, 3584], P(None, ('tp', 'dp')), may hold values from 0.5 to 8
Outputs:
- input_grad: bfloat16 [3072, 3584], P('dp', 'tp')
- master_next: float32 [3, 2048, 3584], P(None, ('tp', 'dp'))
- moment_one_next: float32 [3, 2048, 3584], P(None, ('tp', 'dp'))
- moment_two_next: float32 [3, 2048, 3584], P(None, ('tp', 'dp'))
Inputs may be any that keep to these rules, and one draw needn't show every extreme that they name: `degraded`: exactly 4 replicas have the value 1. `block_map`: in every row the 16 blocks lie on 1 distinct devices, each of which holds 16 or 16 of them, and at least one holds 16. A row is read only where degraded is 1.
All inputs are finite; a program needn't handle non-finite values.
Results may differ from a plain program's by a relative error of at most 0.0075.
Values may be sent and summed in bfloat16 or wider, within the bound.
No kernel may reach another device: no remote copies, remote signals or barrier semaphores. Data moves between devices by JAX's collectives and lax.ppermute only.
A program may use at most 128 MiB of HBM per device.

v0:
```python
import jax
import jax.numpy as jnp
from jax import lax
from jax.experimental import pallas as pl
from jax.experimental.pallas import tpu as pltpu
from jax.sharding import PartitionSpec as P

BLOCK = 128
BLOCKS = 16


beta_one = 0.9
beta_two = 0.95
learn_rate = 0.05
decay_rate = 0.1
adam_eps = 1e-08
bias_one = 1.0 - 0.9**10
bias_two = 1.0 - 0.95**10


def layout_places(replica_flag, mapping, tp_size, slot_count):
    blocks = jnp.arange(BLOCKS, dtype=jnp.int32)
    canonical = blocks // (BLOCKS // tp_size)
    holder = jnp.where(replica_flag > 0, mapping, canonical)
    earlier = (holder[None, :] == holder[:, None]) & (blocks[None, :] < blocks[:, None])
    slot_rank = jnp.sum(earlier.astype(jnp.int32), axis=1)
    return holder * slot_count + slot_rank


def per_device(tokens, cotangent, working, degraded, block_map, master, moment_one, moment_two):
    tp_size = lax.axis_size("tp")
    replicas = lax.axis_size("dp")
    my_index = lax.axis_index("tp")
    weights = working[0, 0]
    slot_count = weights.shape[1] // BLOCK
    per_dev = BLOCKS // tp_size
    places = layout_places(degraded[0], block_map[0], tp_size, slot_count)
    my_slots = my_index * slot_count + jnp.arange(slot_count, dtype=jnp.int32)
    holding = places[:, None] == my_slots[None, :]
    filled = jnp.any(holding, axis=0).astype(jnp.float32)
    column_mask = jnp.repeat(filled, BLOCK)
    inputs, upstream = (
        lax.all_gather(tokens, "tp", axis=1, tiled=True),
        lax.all_gather(cotangent, "tp", axis=1, tiled=True),
    )
    contract_d = (((1,), (1,)), ((), ()))
    gate_pre = lax.dot_general(inputs, weights[0], contract_d, preferred_element_type=jnp.float32)
    up_pre = lax.dot_general(inputs, weights[1], contract_d, preferred_element_type=jnp.float32)
    hidden_grad = lax.dot_general(
        upstream, weights[2], contract_d, preferred_element_type=jnp.float32
    )
    gate_sig = jax.nn.sigmoid(gate_pre)
    active = gate_pre * gate_sig
    hidden = (active * up_pre * column_mask).astype(jnp.bfloat16)
    gate_grad = (
        hidden_grad * up_pre * gate_sig * (1.0 + gate_pre * (1.0 - gate_sig)) * column_mask
    ).astype(jnp.bfloat16)
    up_grad = (hidden_grad * active * column_mask).astype(jnp.bfloat16)
    partial_value = jnp.dot(gate_grad, weights[0], preferred_element_type=jnp.float32) + jnp.dot(
        up_grad, weights[1], preferred_element_type=jnp.float32
    )
    input_grad = lax.psum_scatter(partial_value, "tp", scatter_dimension=1, tiled=True).astype(
        jnp.bfloat16
    )
    tok_rows = gate_grad.shape[0]
    packed = jnp.stack(
        [
            hidden.reshape(tok_rows, slot_count, BLOCK),
            gate_grad.reshape(tok_rows, slot_count, BLOCK),
            up_grad.reshape(tok_rows, slot_count, BLOCK),
        ],
        axis=2,
    )
    packed = packed.transpose(1, 0, 2, 3).reshape(slot_count, tok_rows, 3 * BLOCK)
    selector = holding.astype(jnp.bfloat16)
    outgoing = jnp.einsum(
        "qs,stc->qtc", selector, packed, preferred_element_type=jnp.float32
    ).astype(jnp.bfloat16)
    incoming = lax.all_to_all(outgoing, "tp", split_axis=0, concat_axis=0, tiled=True)
    owned_acts = jnp.sum(incoming.reshape(tp_size, per_dev, tok_rows, 3 * BLOCK), axis=0)
    owned_kinds = (
        owned_acts.reshape(per_dev, tok_rows, 3, BLOCK)
        .transpose(2, 1, 0, 3)
        .reshape(3, tok_rows, per_dev * BLOCK)
    )
    contract_t = (((0,), (0,)), ((), ()))
    gate_term = lax.dot_general(
        owned_kinds[1], inputs, contract_t, preferred_element_type=jnp.float32
    )
    up_term = lax.dot_general(
        owned_kinds[2], inputs, contract_t, preferred_element_type=jnp.float32
    )
    down_term = lax.dot_general(
        owned_kinds[0], upstream, contract_t, preferred_element_type=jnp.float32
    )
    summed = lax.psum_scatter(
        jnp.stack([gate_term, up_term, down_term], axis=1).astype(jnp.bfloat16),
        "dp",
        scatter_dimension=0,
        tiled=True,
    ).astype(jnp.float32)
    grad_mean = jnp.transpose(summed, (1, 0, 2)) / replicas
    moment_one_next = beta_one * moment_one + (1.0 - beta_one) * grad_mean
    moment_two_next = beta_two * moment_two + (1.0 - beta_two) * grad_mean * grad_mean
    update = (
        moment_one_next / bias_one / (jnp.sqrt(moment_two_next / bias_two) + adam_eps)
        + decay_rate * master
    )
    master_next = master - learn_rate * update
    return (input_grad, master_next, moment_one_next, moment_two_next)


CORES = 2
WIDE = 4 * BLOCK
contract_last = (((1,), (1,)), ((), ()))
contract_mid = (((1,), (0,)), ((), ()))


def dot32(a, b, dims):
    return lax.dot_general(a, b, dims, preferred_element_type=jnp.float32)


FLAG, HOLDER, ME, CORE, NEAR = range(5)


def group_of(i, s, tp_size, depth):
    owner = (s[ME] + 1 + i // depth) % tp_size
    held = jnp.where(s[FLAG] > 0, s[HOLDER] == s[ME], owner == s[ME])
    place = jnp.where(s[FLAG] > 0, owner * depth + i % depth, i % depth)
    return held, jnp.where(held, place, 0)


def weight_specs(kinds, half, sides, layout):
    def spec(kind, side):
        def where(i, s):
            _, place = group_of(i, s, *layout)
            return (0, 0, kind, place, s[ME] if side == 0 else 1 - s[ME])

        return pl.BlockSpec((1, 1, 1, WIDE, half), where)

    return [spec(kind, side) for kind in kinds for side in sides]


def whole_spec(shape):
    return pl.BlockSpec(shape, lambda *_: (0,) * len(shape))


def step_spec(rows):
    return pl.BlockSpec((1, rows, WIDE), lambda i, s: (i, 0, 0))


def own_part(scalars, tokens, cotangent, working, layout):
    steps = layout[0] * layout[1]
    rows, half = tokens.shape

    def body(s, t_ref, c_ref, *refs):
        weights, outs = refs[:3], refs[3:]
        held, _ = group_of(pl.program_id(0), s, *layout)

        @pl.when(held)
        def _():
            for kind, out in enumerate(outs):
                left = c_ref if kind == 2 else t_ref
                out[0] = dot32(left[...], weights[kind][0, 0, 0], contract_last)

    out = jax.ShapeDtypeStruct((steps, rows, WIDE), jnp.float32)
    return pl.pallas_call(
        body,
        out_shape=(out,) * 3,
        grid_spec=pltpu.PrefetchScalarGridSpec(
            num_scalar_prefetch=1,
            grid=(steps,),
            in_specs=[whole_spec(tokens.shape)] * 2 + weight_specs((0, 1, 2), half, (0,), layout),
            out_specs=(step_spec(rows),) * 3,
        ),
        cost_estimate=pl.CostEstimate(
            flops=6 * rows * half * steps * WIDE, bytes_accessed=6 * half * steps * WIDE, transcendentals=0
        ),
        name="own_part",
    )(scalars, tokens, cotangent, *[working] * 3)


def act_outputs(layout, kinds, rows):
    depth = layout[1]
    block = (2, CORES, 1, kinds, rows, BLOCK)
    shape = jax.ShapeDtypeStruct((2, CORES, depth, kinds, rows, BLOCK), jnp.bfloat16)
    specs = (
        pl.BlockSpec(block, lambda i, s: (0, 0, jnp.minimum(i, depth - 1), 0, 0, 0)),
        pl.BlockSpec(block, lambda i, s: (0, 0, jnp.maximum(i - depth, 0), 0, 0, 0)),
    )
    return (shape, shape), specs


def put_acts(i, s, layout, values, theirs, mine):
    narrow = BLOCK // CORES

    def put(ref):
        for kind, value in enumerate(values):
            for side in range(2):
                for c in range(CORES):
                    starts = [(side * 2 + j) * BLOCK + c * narrow for j in range(2)]
                    piece = jnp.concatenate([value[:, at : at + narrow] for at in starts], axis=1)
                    ref[jnp.bitwise_xor(s[NEAR], side), jnp.bitwise_xor(s[CORE], c), 0, kind] = piece.astype(
                        jnp.bfloat16
                    )

    pl.when(i < layout[1])(lambda: put(theirs))
    pl.when(i >= layout[1])(lambda: put(mine))


def clear_acts(i, layout, theirs, mine):
    def clear(ref):
        ref[...] = jnp.zeros(ref.shape, ref.dtype)

    pl.when(i < layout[1])(lambda: clear(theirs))
    pl.when(i >= layout[1])(lambda: clear(mine))


def gate_up(scalars, other, working, gate, up, layout):
    steps = layout[0] * layout[1]
    rows, half = other.shape

    def body(s, other_ref, w0, w1, gate_ref, up_ref, act_ref, slope_ref, *outs):
        i = pl.program_id(0)
        held, _ = group_of(i, s, *layout)

        @pl.when(held)
        def _():
            zg = gate_ref[0] + dot32(other_ref[...], w0[0, 0, 0], contract_last)
            zu = up_ref[0] + dot32(other_ref[...], w1[0, 0, 0], contract_last)
            sig = jax.nn.sigmoid(zg)
            act = zg * sig
            act_ref[0] = act
            slope_ref[0] = zu * sig * (1.0 + zg * (1.0 - sig))
            put_acts(i, s, layout, [act * zu], *outs)

        pl.when(jnp.logical_not(held))(lambda: clear_acts(i, layout, *outs))

    out = jax.ShapeDtypeStruct((steps, rows, WIDE), jnp.float32)
    shapes, specs = act_outputs(layout, 1, rows)
    return pl.pallas_call(
        body,
        out_shape=(out, out, *shapes),
        grid_spec=pltpu.PrefetchScalarGridSpec(
            num_scalar_prefetch=1,
            grid=(steps,),
            in_specs=[whole_spec(other.shape)] + weight_specs((0, 1), half, (1,), layout) + [step_spec(rows)] * 2,
            out_specs=(step_spec(rows), step_spec(rows), *specs),
        ),
        cost_estimate=pl.CostEstimate(
            flops=4 * rows * half * steps * WIDE,
            bytes_accessed=4 * half * steps * WIDE + 16 * rows * steps * WIDE,
            transcendentals=rows * steps * WIDE,
        ),
        name="gate_up",
    )(scalars, other, *[working] * 2, gate, up)


def down_acts(scalars, other, working, partial, act, slope, layout):
    steps = layout[0] * layout[1]
    rows, half = other.shape

    def body(s, other_ref, w0, partial_ref, act_ref, slope_ref, grads, *outs):
        i = pl.program_id(0)
        held, _ = group_of(i, s, *layout)

        @pl.when(held)
        def _():
            dh = partial_ref[0] + dot32(other_ref[...], w0[0, 0, 0], contract_last)
            dgate = dh * slope_ref[0]
            dup = dh * act_ref[0]
            grads[0, 0] = dgate.astype(jnp.bfloat16)
            grads[0, 1] = dup.astype(jnp.bfloat16)
            put_acts(i, s, layout, [dgate, dup], *outs)

        pl.when(jnp.logical_not(held))(lambda: clear_acts(i, layout, *outs))

    shapes, specs = act_outputs(layout, 2, rows)
    return pl.pallas_call(
        body,
        out_shape=(jax.ShapeDtypeStruct((steps, 2, rows, WIDE), jnp.bfloat16), *shapes),
        grid_spec=pltpu.PrefetchScalarGridSpec(
            num_scalar_prefetch=1,
            grid=(steps,),
            in_specs=[whole_spec(other.shape)] + weight_specs((2,), half, (1,), layout) + [step_spec(rows)] * 3,
            out_specs=(pl.BlockSpec((1, 2, rows, WIDE), lambda i, s: (i, 0, 0, 0)), *specs),
        ),
        cost_estimate=pl.CostEstimate(
            flops=2 * rows * half * steps * WIDE,
            bytes_accessed=2 * half * steps * WIDE + 20 * rows * steps * WIDE,
            transcendentals=0,
        ),
        name="down_acts",
    )(scalars, other, working, partial, act, slope)


def input_part(scalars, grads, working, half, side, layout):
    steps = layout[0] * layout[1]
    rows = grads.shape[2]

    def body(s, grads_ref, w0, w1, out_ref, total):
        i = pl.program_id(0)
        held, _ = group_of(i, s, *layout)

        @pl.when(i == 0)
        def _():
            total[...] = jnp.zeros(total.shape, total.dtype)

        @pl.when(held)
        def _():
            total[...] += dot32(grads_ref[0, 0], w0[0, 0, 0], contract_mid) + dot32(
                grads_ref[0, 1], w1[0, 0, 0], contract_mid
            )

        @pl.when(i == steps - 1)
        def _():
            out_ref[...] = total[...].astype(out_ref.dtype)

    return pl.pallas_call(
        body,
        out_shape=jax.ShapeDtypeStruct((rows, half), jnp.bfloat16 if side else jnp.float32),
        grid_spec=pltpu.PrefetchScalarGridSpec(
            num_scalar_prefetch=1,
            grid=(steps,),
            in_specs=[pl.BlockSpec((1, 2, rows, WIDE), lambda i, s: (i, 0, 0, 0))]
            + weight_specs((0, 1), half, (side,), layout),
            out_specs=whole_spec((rows, half)),
            scratch_shapes=[pltpu.VMEM((rows, half), jnp.float32)],
        ),
        cost_estimate=pl.CostEstimate(
            flops=4 * rows * half * steps * WIDE, bytes_accessed=4 * half * steps * WIDE, transcendentals=0
        ),
        name="input_other" if side else "input_own",
    )(scalars, grads, *[working] * 2)


def weight_grad(acts, inputs, own):
    group = len(acts)
    depth, kinds, rows, _ = acts[0].shape[-4:]
    half = inputs[0].shape[1]
    narrow = BLOCK // CORES
    wide = depth * BLOCK
    owners = wide // narrow
    tile = half // 2 if half % (2 * BLOCK) == 0 else half

    def body(s, *refs):
        a_refs, x_refs, outs = refs[:group], refs[group : 2 * group], refs[2 * group : 2 * group + kinds * owners]
        left, value = refs[2 * group + kinds * owners :]

        @pl.when(pl.program_id(0) == 0)
        def _():
            for kind in range(kinds):
                for p in range(depth):
                    column = jnp.concatenate(
                        [ref[0, p, kind] if len(ref.shape) == 5 else ref[p, kind] for ref in a_refs], axis=0
                    )
                    left[kind, p * BLOCK : (p + 1) * BLOCK, :] = column.T

        right = jnp.concatenate([ref[...] for ref in x_refs], axis=0)
        for kind in range(kinds):
            value[...] = dot32(left[kind], right, contract_mid).astype(jnp.bfloat16)
            for relation in range(owners):
                start = pl.multiple_of(jnp.bitwise_xor(s[0], relation) * narrow, narrow)
                outs[kind * owners + relation][...] = value[pl.ds(start, narrow), :]

    def act_spec(a):
        if a.ndim == 5:
            return pl.BlockSpec((1, *a.shape[1:]), lambda i, s: (0,) * 5)
        return pl.BlockSpec(a.shape, lambda i, s: (0,) * 4)

    out = jax.ShapeDtypeStruct((narrow, half), jnp.bfloat16)
    made = pl.pallas_call(
        body,
        out_shape=(out,) * (kinds * owners),
        grid_spec=pltpu.PrefetchScalarGridSpec(
            num_scalar_prefetch=1,
            grid=(half // tile,),
            in_specs=[act_spec(a) for a in acts] + [pl.BlockSpec((rows, tile), lambda i, s: (0, i))] * group,
            out_specs=(pl.BlockSpec((narrow, tile), lambda i, s: (0, i)),) * (kinds * owners),
            scratch_shapes=[
                pltpu.VMEM((kinds, wide, group * rows), jnp.bfloat16),
                pltpu.VMEM((wide, tile), jnp.bfloat16),
            ],
        ),
        cost_estimate=pl.CostEstimate(
            flops=2 * kinds * group * rows * wide * half,
            bytes_accessed=2 * group * rows * half + 2 * kinds * wide * half,
            transcendentals=0,
        ),
    )(own, *acts, *inputs)
    return [made[kind * owners : (kind + 1) * owners] for kind in range(kinds)]


def adam(me, sums, kinds, halves, master, moment_one, moment_two, before, replicas):
    rows, half = sums[0][0].shape
    count = len(sums[0])
    steps = len(sums)
    columns = master.shape[2] // half

    def at(i, s):
        kind = kinds[0] + i * (kinds[1] - kinds[0])
        return (kind, 0, (s[0] + halves[0] + i * (halves[1] - halves[0])) % columns)

    state = pl.BlockSpec((1, rows, half), at)

    def body(s, *refs):
        parts, (master_ref, one_ref, two_ref) = refs[: steps * count], refs[steps * count : steps * count + 3]
        master_out, one_out, two_out = refs[-3:]
        for i in range(steps):

            @pl.when(pl.program_id(0) == i)
            def _(i=i):
                summed = parts[i * count][...].astype(jnp.float32)
                for part in parts[i * count + 1 : (i + 1) * count]:
                    summed = summed + part[...].astype(jnp.float32)
                grad_mean = summed * (1.0 / replicas)
                one = beta_one * one_ref[0] + (1.0 - beta_one) * grad_mean
                two = beta_two * two_ref[0] + (1.0 - beta_two) * grad_mean * grad_mean
                old = master_ref[0]
                update = one * (1.0 / bias_one) / (jnp.sqrt(two * (1.0 / bias_two)) + adam_eps) + decay_rate * old
                master_out[0] = old - learn_rate * update
                one_out[0] = one
                two_out[0] = two

    extra = () if before is None else before
    flat = [part for group in sums for part in group]
    return pl.pallas_call(
        body,
        out_shape=(jax.ShapeDtypeStruct(master.shape, jnp.float32),) * 3,
        grid_spec=pltpu.PrefetchScalarGridSpec(
            num_scalar_prefetch=1,
            grid=(steps,),
            in_specs=[pl.BlockSpec((rows, half), lambda i, s: (0, 0))] * len(flat)
            + [state] * 3
            + [pl.BlockSpec(memory_space=pl.ANY)] * len(extra),
            out_specs=(state,) * 3,
        ),
        input_output_aliases={len(flat) + 4 + i: i for i in range(len(extra))},
        cost_estimate=pl.CostEstimate(
            flops=20 * steps * rows * half, bytes_accessed=28 * steps * rows * half, transcendentals=0
        ),
        name="adam",
    )(me, *flat, master, moment_one, moment_two, *extra)


def grouped(*args):
    return grouped_step(*args)


def grouped_step(tokens, cotangent, working, degraded, block_map, master, moment_one, moment_two):
    replicas = lax.axis_size("dp")
    tp_size = lax.axis_size("tp")
    me = lax.axis_index("tp")
    mine = lax.axis_index("dp")
    core, x = mine % CORES, (mine // CORES) % 2
    zs, zp = (mine // (2 * CORES)) % 2, mine // (4 * CORES)
    per_dev = BLOCKS // tp_size
    half = tokens.shape[1]
    after = lax.optimization_barrier

    def over_y(v):
        return lax.ppermute(v, "tp", [(i, (i + 1) % tp_size) for i in range(tp_size)])

    def over(bit, v):
        pairs = [(i, i ^ bit) for i in range(replicas)]
        return lax.ppermute(v, "dp", pairs)

    def over_core(v):
        return over(1, v)

    def over_x(v):
        return over(CORES, v)

    def over_s(v):
        return over(2 * CORES, v)

    def over_m(v):
        return over(4 * CORES, v)

    layout = (tp_size, per_dev * BLOCK // WIDE)
    scalars = jnp.stack([degraded[0], block_map[0, 0], me, core, zs]).astype(jnp.int32)
    own = (zp * 2 + x).astype(jnp.int32).reshape(1)

    t_own, c_own = tokens, cotangent
    t_other = over_y(t_own)
    c_own_s = over_s(c_own)
    t_own_s = over_s(t_own)
    gate, up, down = own_part(scalars, t_own, c_own, working, layout)
    t_other, c_first = after((t_other, c_own))
    c_other = over_y(c_first)
    c_own_c, t_own_c = over_core(c_own), over_core(t_own)
    act, slope, h_theirs, h_mine = gate_up(scalars, t_other, working, gate, up, layout)
    c_other, h_theirs = after((c_other, h_theirs))
    h_from = over_y(h_theirs)
    c_other_s = over_s(c_other)
    grads, d_theirs, d_mine = down_acts(scalars, c_other, working, down, act, slope, layout)
    h_from, d_theirs = after((h_from, d_theirs))
    d_from = over_y(d_theirs)

    def spread(mine, came):
        far = mine[1] + came[1]
        near_s = over_s(far)
        near = mine[0] + came[0]
        return [near, near_s, over_core(near[1]), over_core(near_s[1])]

    hidden_acts = spread(h_mine, h_from)
    t_other_s = over_s(t_other)
    c_acts = [
        [c_own, c_own_s, c_own_c, over_core(c_own_s)], [c_other, c_other_s, over_core(c_other), over_core(c_other_s)]
    ]
    t_acts = [
        [t_own, t_own_s, t_own_c, over_core(t_own_s)], [t_other, t_other_s, over_core(t_other), over_core(t_other_s)]
    ]
    grad_acts = spread(d_mine, d_from)

    made = []
    for h in range(2):
        made += weight_grad(hidden_acts, c_acts[h], own)
    for h in range(2):
        made += weight_grad(grad_acts, t_acts[h], own)
    sums = []
    for keep, far_x, far_z, far_both in made:
        came = over_x(far_both)
        far_z = (far_z.astype(jnp.float32) + came.astype(jnp.float32)).astype(jnp.bfloat16)
        sums.append((keep, over_x(far_x), over_m(far_z)))
    state = None
    for at in range(0, len(PIECES), 2):
        kinds, halves = zip(*PIECES[at : at + 2])
        state = adam(
            me.astype(jnp.int32).reshape(1),
            sums[at : at + 2],
            kinds,
            halves,
            master,
            moment_one,
            moment_two,
            state,
            replicas,
        )

    sent = over_y(input_part(scalars, grads, working, half, 1, layout))
    kept = input_part(scalars, grads, working, half, 0, layout)
    input_grad = (kept + sent.astype(jnp.float32)).astype(jnp.bfloat16)
    return (input_grad, *state)


PIECES = ((2, 0), (2, 1), (0, 0), (1, 0), (0, 1), (1, 1))


def solution(mesh):
    replicas, tp_size = mesh.shape["dp"], mesh.shape["tp"]

    def per_part(*args):
        half = args[0].shape[1]
        rows = args[5].shape[1]
        whole = args[2].shape[3] == BLOCKS * BLOCK
        aligned = half % BLOCK == 0 and args[0].shape[0] % 16 == 0 and rows * CORES == BLOCK
        split = replicas == 8 * CORES and tp_size == 2 and BLOCKS == tp_size * replicas // CORES
        return (grouped if whole and aligned and split else per_device)(*args)

    return jax.shard_map(
        per_part,
        mesh=mesh,
        in_specs=(
            P("dp", "tp"),
            P("dp", "tp"),
            P("dp", "tp", None, None, None),
            P("dp"),
            P("dp", None),
            P(None, ("tp", "dp"), None),
            P(None, ("tp", "dp"), None),
            P(None, ("tp", "dp"), None),
        ),
        out_specs=(
            P("dp", "tp"),
            P(None, ("tp", "dp"), None),
            P(None, ("tp", "dp"), None),
            P(None, ("tp", "dp"), None),
        ),
        check_vma=False,
    )
```

profile of v0, /device:TPU:0, one launch (start us, length us, event | category | flops | bytes accessed | tf_op | source)
XLA Modules:
  0.0 214.6 jit_solution(10547582788550233174)
XLA Ops:
  0.6 3.1 %collective-permute-start = (bf16[192,1792]{1,0:T(8,128)(2,1)}, bf16[192,1792]{1,0:T(8,128)(2,1)}, u32[]{:S(2)}, u32[]{:S(2)}) collective-permute-start(bf16[192,1792]{1,0:T(8,128)(2,1)} %refs_4_.2), channel_id=1, source_target_pairs={{0,1},{1,0},{2,3},{3,2},{4,5},{5,4},{6,7},{7,6},{8,9},{9,8},{10,11... | collective-permute-start | bytes 2064392 | tf_op jit(solution)/shard_map/ppermute | solution.py:462
  3.7 15.8 %collective-permute-done.other_ref.refs_4_ = bf16[192,1792]{1,0:T(8,128)(2,1)} collective-permute-done((bf16[192,1792]{1,0:T(8,128)(2,1)}, bf16[192,1792]{1,0:T(8,128)(2,1)}, u32[]{:S(2)}, u32[]{:S(2)}) %collective-permute-start) | collective-permute-done | bytes 688160 | tf_op jit(solution)/shard_map/ppermute | solution.py:462
  19.4 1.7 collective-permute-start.1
  21.2 1.6 collective-permute-start.17
  22.8 0.4 collective-permute-start.29
  23.9 1.3 stack.15.s
  25.2 10.2 %own_part.1 = (f32[4,192,512]{2,1,0:T(8,128)}, f32[4,192,512]{2,1,0:T(8,128)}, f32[4,192,512]{2,1,0:T(8,128)}) custom-call(s32[5]{0:T(128)} %stack.15.s, bf16[192,1792]{1,0:T(8,128)(2,1)} %refs_4_.2, bf16[192,1792]{1,0:T(8,128)(2,1)} %refs_4_.3, bf16[1,1,3,2048,3584]{4,3,2,1,0:T(8,128)(2,1)} %w1.5, bf16[1,1,3,2048,3584]{4,3,2,1,0:T(8,128)(2,1)} %w1.5, ...), custom_call_target="tpu_custom_call" | custom-call | flops 4227858432 | bytes 22020096 | tf_op jit(solution)/shard_map/own_part/pallas_call | solution.py:167
  35.4 9.3 %gate_up.1 = (f32[4,192,512]{2,1,0:T(8,128)}, f32[4,192,512]{2,1,0:T(8,128)}, bf16[2,2,2,1,192,128]{5,4,3,2,1,0:T(8,128)(2,1)}, bf16[2,2,2,1,192,128]{5,4,3,2,1,0:T(8,128)(2,1)}) custom-call(s32[5]{0:T(128)} %stack.15.s, bf16[192,1792]{1,0:T(8,128)(2,1)} %collective-permute-done.other_ref.refs_4_, bf16[1,1,3,2048,3584]{4,3,2,1,0:T(8,128)(2,1)} %w1.5, ...), custom_call_target="tpu_custom_call" | custom-call | flops 2818572288 | bytes 20971520 | tf_op jit(solution)/shard_map/gate_up/pallas_call | solution.py:241
  45.0 5.2 %collective-permute-start.30 = (bf16[192,1792]{1,0:T(8,128)(2,1)S(1)}, bf16[192,1792]{1,0:T(8,128)(2,1)}, u32[]{:S(2)}, u32[]{:S(2)}) collective-permute-start(bf16[192,1792]{1,0:T(8,128)(2,1)S(1)} %copy-done.1), channel_id=1, source_target_pairs={{0,2},{2,0},{4,6},{6,4},{8,10},{10,8},{12,14},{14,12},{16,18},{18,... | collective-permute-start | bytes 2064392 | tf_op jit(solution)/shard_map/ppermute | solution.py:466
  50.3 3.6 %collective-permute-start.8 = (bf16[192,1792]{1,0:T(8,128)(2,1)}, bf16[192,1792]{1,0:T(8,128)(2,1)}, u32[]{:S(2)}, u32[]{:S(2)}) collective-permute-start(bf16[192,1792]{1,0:T(8,128)(2,1)} %collective-permute-done.other_ref.refs_4_), channel_id=1, source_target_pairs={{0,8},{2,10},{4,12},{6,14},{8,0},{10,2},{12,4},{14,6},{16,24},{18,... | collective-permute-start | bytes 2064392 | tf_op jit(solution)/shard_map/ppermute | solution.py:466
  53.9 7.8 %down_acts.1 = (bf16[4,2,192,512]{3,2,1,0:T(8,128)(2,1)}, bf16[2,2,2,2,192,128]{5,4,3,2,1,0:T(8,128)(2,1)}, bf16[2,2,2,2,192,128]{5,4,3,2,1,0:T(8,128)(2,1)}) custom-call(s32[5]{0:T(128)} %stack.15.s, bf16[192,1792]{1,0:T(8,128)(2,1)} %copy-done.2, bf16[1,1,3,2048,3584]{4,3,2,1,0:T(8,128)(2,1)} %w1.5, f32[4,192,512]{2,1,0:T(8,128)} %get-tuple-element.59.partial_ref, ...), custom_call_target="tpu_custom_call" | custom-call | flops 1409286144 | bytes 15204352 | tf_op jit(solution)/shard_map/down_acts/pallas_call | solution.py:279
  62.0 2.1 collective-permute-start.35
  64.2 0.8 copy-done.9
  65.0 7.3 %input_other.1 = bf16[192,1792]{1,0:T(8,128)(2,1)} custom-call(s32[5]{0:T(128)} %stack.15.s, bf16[4,2,192,512]{3,2,1,0:T(8,128)(2,1)} %get-tuple-element.62.grads_ref, bf16[1,1,3,2048,3584]{4,3,2,1,0:T(8,128)(2,1)} %w1.5, bf16[1,1,3,2048,3584]{4,3,2,1,0:T(8,128)(2,1)} %w1.5), custom_call_target="tpu_custom_call" | custom-call | flops 2818572288 | bytes 14680064 | tf_op jit(solution)/shard_map/input_other/pallas_call | solution.py:319
  72.2 17.0 %collective-permute-done.26 = bf16[2,2,1,192,128]{4,3,1,2,0:T(8,128)(2,1)S(1)} collective-permute-done((bf16[2,2,1,192,128]{4,3,1,2,0:T(8,128)(2,1)S(1)}, bf16[2,2,1,192,128]{4,3,1,2,0:T(8,128)(2,1)S(1)}, u32[]{:S(2)}, u32[]{:S(2)}) %collective-permute-start.26) | collective-permute-done | bytes 196640 | tf_op jit(solution)/shard_map/ppermute | solution.py:466
  89.2 0.6 collective-permute-start.36
  89.9 0.4 collective-permute-start.28
  90.4 1.2 fusion
  91.7 0.5 collective-permute-start.9
  92.1 0.5 collective-permute-done.27
  92.8 1.7 collective-permute-start.5
  94.6 7.4 %input_own.1 = f32[192,1792]{1,0:T(8,128)} custom-call(s32[5]{0:T(128)} %stack.15.s, bf16[4,2,192,512]{3,2,1,0:T(8,128)(2,1)} %get-tuple-element.62.grads_ref, bf16[1,1,3,2048,3584]{4,3,2,1,0:T(8,128)(2,1)} %w1.5, bf16[1,1,3,2048,3584]{4,3,2,1,0:T(8,128)(2,1)} %w1.5), custom_call_target="tpu_custom_call" | custom-call | flops 2818572288 | bytes 14680064 | tf_op jit(solution)/shard_map/input_own/pallas_call | solution.py:319
  102.0 3.8 %shard_map.113 = (bf16[64,1792]{1,0:T(8,128)(2,1)}, bf16[64,1792]{1,0:T(8,128)(2,1)}, bf16[64,1792]{1,0:T(8,128)(2,1)}, bf16[64,1792]{1,0:T(8,128)(2,1)}) custom-call(s32[1]{0:T(128)} %bitcast.4.s, bf16[2,2,1,192,128]{4,3,2,1,0:T(8,128)(2,1)} %bitcast.26, bf16[2,2,1,192,128]{4,3,2,1,0:T(8,128)(2,1)} %bitcast.28, bf16[2,1,192,128]{3,2,1,0:T(8,128)(2,1)} %bitcast.32, ...), custom_call_target="tpu_custom_call" | custom-call | flops 704643072 | bytes 3670016 | tf_op jit(solution)/shard_map/pallas_call | solution.py:372
  105.8 0.7 slice_bitcast_fusion.1
  106.6 0.5 collective-permute-start.19
  107.0 3.8 %shard_map.114 = (bf16[64,1792]{1,0:T(8,128)(2,1)}, bf16[64,1792]{1,0:T(8,128)(2,1)}, bf16[64,1792]{1,0:T(8,128)(2,1)}, bf16[64,1792]{1,0:T(8,128)(2,1)}) custom-call(s32[1]{0:T(128)} %bitcast.4.s, bf16[2,2,1,192,128]{4,3,2,1,0:T(8,128)(2,1)} %bitcast.27, bf16[2,2,1,192,128]{4,3,2,1,0:T(8,128)(2,1)} %bitcast.29, bf16[2,1,192,128]{3,2,1,0:T(8,128)(2,1)} %bitcast.33, ...), custom_call_target="tpu_custom_call" | custom-call | flops 704643072 | bytes 3670016 | tf_op jit(solution)/shard_map/pallas_call | solution.py:372
  110.9 0.9 slice_bitcast_fusion
  112.0 2.0 collective-permute-start.39
  114.1 5.3 %collective-permute-done.33 = bf16[64,1792]{1,0:T(8,128)(2,1)S(1)} collective-permute-done((bf16[64,1792]{1,0:T(8,128)(2,1)S(1)}, bf16[64,1792]{1,0:T(8,128)(2,1)S(1)}, u32[]{:S(2)}, u32[]{:S(2)}) %collective-permute-start.33) | collective-permute-done | bytes 229408 | tf_op jit(solution)/shard_map/ppermute | solution.py:466
  119.4 0.7 add_convert_fusion.2
  120.2 2.0 collective-permute-start.2
  122.1 0.7 copy-done.27
  122.8 4.8 %shard_map.111 = (bf16[64,1792]{1,0:T(8,128)(2,1)}, bf16[64,1792]{1,0:T(8,128)(2,1)}, bf16[64,1792]{1,0:T(8,128)(2,1)}, bf16[64,1792]{1,0:T(8,128)(2,1)}, bf16[6...) custom-call(s32[1]{0:T(128)} %bitcast.4.s, ...), custom_call_target="tpu_custom_call" | custom-call | flops 1409286144 | bytes 4587520 | tf_op jit(solution)/shard_map/pallas_call | solution.py:372
  127.6 2.1 collective-permute-start.12
  129.7 0.8 add_convert_fusion.1
  130.5 1.6 collective-permute-start.34
  132.1 1.2 collective-permute-start.38
  133.3 4.8 %shard_map.112 = (bf16[64,1792]{1,0:T(8,128)(2,1)}, bf16[64,1792]{1,0:T(8,128)(2,1)}, bf16[64,1792]{1,0:T(8,128)(2,1)}, bf16[64,1792]{1,0:T(8,128)(2,1)}, bf16[6...) custom-call(s32[1]{0:T(128)} %bitcast.4.s, ...), custom_call_target="tpu_custom_call" | custom-call | flops 1409286144 | bytes 4587520 | tf_op jit(solution)/shard_map/pallas_call | solution.py:372
  138.1 0.9 collective-permute-start.15
  139.1 1.1 add_convert_fusion.6
  140.2 5.3 %collective-permute-done.15 = bf16[64,1792]{1,0:T(8,128)(2,1)S(1)} collective-permute-done((bf16[64,1792]{1,0:T(8,128)(2,1)}, bf16[64,1792]{1,0:T(8,128)(2,1)S(1)}, u32[]{:S(2)}, u32[]{:S(2)}) %collective-permute-start.15) | collective-permute-done | bytes 229408 | tf_op jit(solution)/shard_map/ppermute | solution.py:466
  145.5 1.7 collective-permute-start.21
  147.2 1.7 add_convert_fusion.5
  148.9 3.4 %collective-permute-done.21 = bf16[64,1792]{1,0:T(8,128)(2,1)S(1)} collective-permute-done((bf16[64,1792]{1,0:T(8,128)(2,1)}, bf16[64,1792]{1,0:T(8,128)(2,1)S(1)}, u32[]{:S(2)}, u32[]{:S(2)}) %collective-permute-start.21) | collective-permute-done | bytes 229408 | tf_op jit(solution)/shard_map/ppermute | solution.py:466
  152.3 1.7 collective-permute-start.24
  154.0 1.0 add_convert_fusion.4
  155.0 1.7 collective-permute-start.40
  156.7 1.0 collective-permute-start.20
  157.7 1.0 collective-permute-start.23
  158.8 1.3 collective-permute-done.24
  160.0 3.2 %collective-permute-start.22 = (bf16[64,1792]{1,0:T(8,128)(2,1)S(1)}, bf16[64,1792]{1,0:T(8,128)(2,1)S(1)}, u32[]{:S(2)}, u32[]{:S(2)}) collective-permute-start(bf16[64,1792]{1,0:T(8,128)(2,1)S(1)} %add_convert_fusion.4), channel_id=1, source_target_pairs={{0,16},{2,18},{4,20},{6,22},{8,24},{10,26},{12,28},{14,30},{16,0},... | collective-permute-start | bytes 688136 | tf_op jit(solution)/shard_map/ppermute | solution.py:466
  163.2 1.0 add_convert_fusion.3
  164.2 1.2 collective-permute-start.11
  165.4 6.6 %collective-permute-done.40.refs_5_ = bf16[64,1792]{1,0:T(8,128)(2,1)S(1)} collective-permute-done((bf16[64,1792]{1,0:T(8,128)(2,1)}, bf16[64,1792]{1,0:T(8,128)(2,1)S(1)}, u32[]{:S(2)}, u32[]{:S(2)}) %collective-permute-start.40) | collective-permute-done | bytes 229408 | tf_op jit(solution)/shard_map/ppermute | solution.py:466
  172.0 1.0 collective-permute-start.14
  173.1 2.9 %collective-permute-start.16 = (bf16[64,1792]{1,0:T(8,128)(2,1)}, bf16[64,1792]{1,0:T(8,128)(2,1)}, u32[]{:S(2)}, u32[]{:S(2)}) collective-permute-start(bf16[64,1792]{1,0:T(8,128)(2,1)} %add_convert_fusion.5), channel_id=1, source_target_pairs={{0,16},{2,18},{4,20},{6,22},{8,24},{10,26},{12,28},{14,30},{16,0},... | collective-permute-start | bytes 688136 | tf_op jit(solution)/shard_map/ppermute | solution.py:466
  176.0 10.8 %collective-permute-done.22.refs_2_ = bf16[64,1792]{1,0:T(8,128)(2,1)S(1)} collective-permute-done((bf16[64,1792]{1,0:T(8,128)(2,1)S(1)}, bf16[64,1792]{1,0:T(8,128)(2,1)S(1)}, u32[]{:S(2)}, u32[]{:S(2)}) %collective-permute-start.22) | collective-permute-done | bytes 229408 | tf_op jit(solution)/shard_map/ppermute | solution.py:466
  186.8 0.7 copy-done.23
  187.5 1.0 add_convert_fusion
  188.5 4.0 %adam.3 = (f32[3,64,3584]{2,1,0:T(8,128)}, f32[3,64,3584]{2,1,0:T(8,128)}, f32[3,64,3584]{2,1,0:T(8,128)}) custom-call(s32[1]{0:T(128)} %bitcast.1.s, bf16[64,1792]{1,0:T(8,128)(2,1)} %get-tuple-element.85.refs_0_, bf16[64,1792]{1,0:T(8,128)(2,1)} %copy-done.14, bf16[64,1792]{1,0:T(8,128)(2,1)} %copy-done.15, bf16[64,1792]{1,0:T(8,128)(2,1)} %get-tuple-element.89.refs_3_, ...), custom_call_target="tpu_custom_call" | custom-call | flops 4587520 | bytes 6422528 | tf_op jit(solution)/shard_map/adam/pallas_call | solution.py:427
  192.4 13.6 %collective-permute-done.25.refs_5_ = bf16[64,1792]{1,0:T(8,128)(2,1)} collective-permute-done((bf16[64,1792]{1,0:T(8,128)(2,1)S(1)}, bf16[64,1792]{1,0:T(8,128)(2,1)}, u32[]{:S(2)}, u32[]{:S(2)}) %collective-permute-start.25) | collective-permute-done | bytes 229408 | tf_op jit(solution)/shard_map/ppermute | solution.py:466
  206.0 3.9 %adam.4 = (f32[3,64,3584]{2,1,0:T(8,128)}, f32[3,64,3584]{2,1,0:T(8,128)}, f32[3,64,3584]{2,1,0:T(8,128)}) custom-call(s32[1]{0:T(128)} %bitcast.1.s, bf16[64,1792]{1,0:T(8,128)(2,1)} %get-tuple-element.75.refs_0_, bf16[64,1792]{1,0:T(8,128)(2,1)} %copy-done.21, ...), custom_call_target="tpu_custom_call", output_to_operand_aliasing={{0}: (10, {}), {1}: (11, {}), {2}: (12, {})} | custom-call | flops 4587520 | bytes 6422528 | tf_op jit(solution)/shard_map/adam/pallas_call | solution.py:427
  210.0 0.7 copy-done.20
  210.7 3.9 %adam.5 = (f32[3,64,3584]{2,1,0:T(8,128)}, f32[3,64,3584]{2,1,0:T(8,128)}, f32[3,64,3584]{2,1,0:T(8,128)}) custom-call(s32[1]{0:T(128)} %bitcast.1.s, bf16[64,1792]{1,0:T(8,128)(2,1)} %get-tuple-element.67.refs_0_, bf16[64,1792]{1,0:T(8,128)(2,1)} %copy-done.20, ...), custom_call_target="tpu_custom_call", output_to_operand_aliasing={{0}: (10, {}), {1}: (11, {}), {2}: (12, {})} | custom-call | flops 4587520 | bytes 6422528 | tf_op jit(solution)/shard_map/adam/pallas_call | solution.py:427
  (100 shorter events, 1.6 us)
Async XLA Ops:
  0.6 18.8 %collective-permute-start = (bf16[192,1792]{1,0:T(8,128)(2,1)}, bf16[192,1792]{1,0:T(8,128)(2,1)}, u32[]{:S(2)}, u32[]{:S(2)}) collective-permute-start(bf16[192,1792]{1,0:T(8,128)(2,1)} %refs_4_.2), channel_id=1, source_target_pairs={{0,1},{1,0},{2,3},{3,2},{4,5},{5,4},{6,7},{7,6},{8,9},{9,8},{10,11... | collective-permute-start | bytes 2064392 | tf_op jit(solution)/shard_map/ppermute | solution.py:462
  19.4 25.2 %collective-permute-start.1 = (bf16[192,1792]{1,0:T(8,128)(2,1)}, bf16[192,1792]{1,0:T(8,128)(2,1)S(1)}, u32[]{:S(2)}, u32[]{:S(2)}) collective-permute-start(bf16[192,1792]{1,0:T(8,128)(2,1)} %refs_4_.3), channel_id=1, source_target_pairs={{0,1},{1,0},{2,3},{3,2},{4,5},{5,4},{6,7},{7,6},{8,9},{9,8},{10,11... | collective-permute-start | bytes 2064392 | tf_op jit(solution)/shard_map/ppermute | solution.py:462
  21.2 40.8 %collective-permute-start.17 = (bf16[192,1792]{1,0:T(8,128)(2,1)}, bf16[192,1792]{1,0:T(8,128)(2,1)S(1)}, u32[]{:S(2)}, u32[]{:S(2)}) collective-permute-start(bf16[192,1792]{1,0:T(8,128)(2,1)} %refs_4_.2), channel_id=1, source_target_pairs={{0,8},{2,10},{4,12},{6,14},{8,0},{10,2},{12,4},{14,6},{16,24},{18,... | collective-permute-start | bytes 2064392 | tf_op jit(solution)/shard_map/ppermute | solution.py:466
  22.8 41.3 %collective-permute-start.29 = (bf16[192,1792]{1,0:T(8,128)(2,1)}, bf16[192,1792]{1,0:T(8,128)(2,1)S(1)}, u32[]{:S(2)}, u32[]{:S(2)}) collective-permute-start(bf16[192,1792]{1,0:T(8,128)(2,1)} %refs_4_.3), channel_id=1, source_target_pairs={{0,8},{2,10},{4,12},{6,14},{8,0},{10,2},{12,4},{14,6},{16,24},{18,... | collective-permute-start | bytes 2064392 | tf_op jit(solution)/shard_map/ppermute | solution.py:466
  35.4 9.7 %copy-start.1 = (bf16[192,1792]{1,0:T(8,128)(2,1)S(1)}, bf16[192,1792]{1,0:T(8,128)(2,1)}, u32[]{:S(2)}) copy-start(bf16[192,1792]{1,0:T(8,128)(2,1)} %refs_4_.3) | copy-start | bytes 2064388
  44.7 9.2 %copy-start.2 = (bf16[192,1792]{1,0:T(8,128)(2,1)}, bf16[192,1792]{1,0:T(8,128)(2,1)S(1)}, u32[]{:S(2)}) copy-start(bf16[192,1792]{1,0:T(8,128)(2,1)S(1)} %collective-permute-done.1.other_ref.refs_4_) | copy-start | bytes 2064388
  44.7 17.0 %collective-permute-start.3 = (bf16[2,2,2,1,192,128]{5,4,2,1,3,0:T(8,128)(2,1)}, bf16[2,2,2,1,192,128]{5,4,2,1,3,0:T(8,128)(2,1)S(1)}, u32[]{:S(2)}, u32[]{:S(2)}) collective-permute-start(bf16[2,2,2,1,192,128]{5,4,2,1,3,0:T(8,128)(2,1)} %bitcast.36), channel_id=1, source_target_pairs={{0,1},{1,0},{2,3},{3,2},{4,5},{5,4},{6,7},{7,6},{8,9},{9,8},{10,11... | collective-permute-start | bytes 1179656 | tf_op jit(solution)/shard_map/ppermute | solution.py:462
  45.0 44.2 %collective-permute-start.30 = (bf16[192,1792]{1,0:T(8,128)(2,1)S(1)}, bf16[192,1792]{1,0:T(8,128)(2,1)}, u32[]{:S(2)}, u32[]{:S(2)}) collective-permute-start(bf16[192,1792]{1,0:T(8,128)(2,1)S(1)} %copy-done.1), channel_id=1, source_target_pairs={{0,2},{2,0},{4,6},{6,4},{8,10},{10,8},{12,14},{14,12},{16,18},{18,... | collective-permute-start | bytes 2064392 | tf_op jit(solution)/shard_map/ppermute | solution.py:466
  50.3 39.6 %collective-permute-start.8 = (bf16[192,1792]{1,0:T(8,128)(2,1)}, bf16[192,1792]{1,0:T(8,128)(2,1)}, u32[]{:S(2)}, u32[]{:S(2)}) collective-permute-start(bf16[192,1792]{1,0:T(8,128)(2,1)} %collective-permute-done.other_ref.refs_4_), channel_id=1, source_target_pairs={{0,8},{2,10},{4,12},{6,14},{8,0},{10,2},{12,4},{14,6},{16,24},{18,... | collective-permute-start | bytes 2064392 | tf_op jit(solution)/shard_map/ppermute | solution.py:466
  53.9 8.0 %copy-start.13 = (bf16[2,2,2,1,192,128]{5,4,3,2,1,0:T(8,128)(2,1)S(1)}, bf16[2,2,2,1,192,128]{5,4,3,2,1,0:T(8,128)(2,1)}, u32[]{:S(2)}) copy-start(bf16[2,2,2,1,192,128]{5,4,3,2,1,0:T(8,128)(2,1)} %get-tuple-element.83) | copy-start | bytes 1179652
  61.7 28.6 %collective-permute-start.4 = (bf16[2,2,2,2,192,128]{5,4,3,2,1,0:T(8,128)(2,1)}, bf16[2,2,2,2,192,128]{5,4,3,2,1,0:T(8,128)(2,1)}, u32[]{:S(2)}, u32[]{:S(2)}) collective-permute-start(bf16[2,2,2,2,192,128]{5,4,3,2,1,0:T(8,128)(2,1)} %get-tuple-element.66), channel_id=1, source_target_pairs={{0,1},{1,0},{2,3},{3,2},{4,5},{5,4},{6,7},{7,6},{8,9},{9,8},{10,11... | collective-permute-start | bytes 2359304 | tf_op jit(solution)/shard_map/ppermute | solution.py:462
  62.0 27.2 %copy-start.4 = (bf16[1,2,2,1,192,128]{5,4,2,1,3,0:T(8,128)(2,1)}, bf16[1,2,2,1,192,128]{5,4,2,1,3,0:T(8,128)(2,1)S(1)}, u32[]{:S(2)}) copy-start(bf16[1,2,2,1,192,128]{5,4,2,1,3,0:T(8,128)(2,1)S(1)} %get-tuple-element.105) | copy-start | bytes 589828
  62.0 2.2 %copy-start.24 = (bf16[192,1792]{1,0:T(8,128)(2,1)}, bf16[192,1792]{1,0:T(8,128)(2,1)S(1)}, u32[]{:S(2)}) copy-start(bf16[192,1792]{1,0:T(8,128)(2,1)S(1)} %collective-permute-done.17.refs_5_) | copy-start | bytes 2064388
  62.0 27.9 %collective-permute-start.35 = (bf16[192,1792]{1,0:T(8,128)(2,1)}, bf16[192,1792]{1,0:T(8,128)(2,1)}, u32[]{:S(2)}, u32[]{:S(2)}) collective-permute-start(bf16[192,1792]{1,0:T(8,128)(2,1)} %copy-done.2), channel_id=1, source_target_pairs={{0,8},{2,10},{4,12},{6,14},{8,0},{10,2},{12,4},{14,6},{16,24},{18,... | collective-permute-start | bytes 2064392 | tf_op jit(solution)/shard_map/ppermute | solution.py:466
  64.1 25.1 %collective-permute-start.26 = (bf16[2,2,1,192,128]{4,3,1,2,0:T(8,128)(2,1)S(1)}, bf16[2,2,1,192,128]{4,3,1,2,0:T(8,128)(2,1)S(1)}, u32[]{:S(2)}, u32[]{:S(2)}) collective-permute-start(bf16[2,2,1,192,128]{4,3,1,2,0:T(8,128)(2,1)S(1)} %get-tuple-element.104), channel_id=1, source_target_pairs={{0,8},{2,10},{4,12},{6,14},{8,0},{10,2},{12,4},{14,6},{16,24},{18,... | collective-permute-start | bytes 589832 | tf_op jit(solution)/shard_map/ppermute | solution.py:466
  65.0 24.3 %copy-start.3 = (bf16[192,1792]{1,0:T(8,128)(2,1)S(1)}, bf16[192,1792]{1,0:T(8,128)(2,1)}, u32[]{:S(2)}) copy-start(bf16[192,1792]{1,0:T(8,128)(2,1)} %copy-done.2) | copy-start | bytes 2064388
  65.0 25.5 %copy-start.7 = (bf16[2,2,2,2,192,128]{5,4,3,2,1,0:T(8,128)(2,1)S(1)}, bf16[2,2,2,2,192,128]{5,4,3,2,1,0:T(8,128)(2,1)}, u32[]{:S(2)}) copy-start(bf16[2,2,2,2,192,128]{5,4,3,2,1,0:T(8,128)(2,1)} %get-tuple-element.63) | copy-start | bytes 2359300
  89.2 12.8 %copy-start.5 = (bf16[2,2,1,192,128]{4,3,1,2,0:T(8,128)(2,1)}, bf16[2,2,1,192,128]{4,3,1,2,0:T(8,128)(2,1)S(1)}, u32[]{:S(2)}) copy-start(bf16[2,2,1,192,128]{4,3,1,2,0:T(8,128)(2,1)S(1)} %collective-permute-done.26) | copy-start | bytes 589828
  89.2 2.5 %collective-permute-start.31 = (bf16[192,1792]{1,0:T(8,128)(2,1)}, bf16[192,1792]{1,0:T(8,128)(2,1)}, u32[]{:S(2)}, u32[]{:S(2)}) collective-permute-start(bf16[192,1792]{1,0:T(8,128)(2,1)} %copy-done.9), channel_id=1, source_target_pairs={{0,2},{2,0},{4,6},{6,4},{8,10},{10,8},{12,14},{14,12},{16,18},{18,... | collective-permute-start | bytes 2064392 | tf_op jit(solution)/shard_map/ppermute | solution.py:466
  89.2 17.2 %collective-permute-start.36 = (bf16[192,1792]{1,0:T(8,128)(2,1)S(1)}, bf16[192,1792]{1,0:T(8,128)(2,1)}, u32[]{:S(2)}, u32[]{:S(2)}) collective-permute-start(bf16[192,1792]{1,0:T(8,128)(2,1)S(1)} %copy-done.3), channel_id=1, source_target_pairs={{0,2},{2,0},{4,6},{6,4},{8,10},{10,8},{12,14},{14,12},{16,18},{18,... | collective-permute-start | bytes 2064392 | tf_op jit(solution)/shard_map/ppermute | solution.py:466
  89.8 2.9 %collective-permute-start.27 = (bf16[2,1,192,128]{3,2,0,1:T(8,128)(2,1)S(1)}, bf16[2,1,192,128]{3,2,0,1:T(8,128)(2,1)S(1)}, u32[]{:S(2)}, u32[]{:S(2)}) collective-permute-start(bf16[2,1,192,128]{3,2,0,1:T(8,128)(2,1)S(1)} %slice_bitcast_fusion.3), channel_id=1, source_target_pairs={{0,2},{2,0},{4,6},{6,4},{8,10},{10,8},{12,14},{14,12},{16,18},{18,... | collective-permute-start | bytes 294920 | tf_op jit(solution)/shard_map/ppermute | solution.py:466
  89.9 2.9 %collective-permute-start.28 = (bf16[2,1,192,128]{3,2,1,0:T(8,128)(2,1)S(1)}, bf16[2,1,192,128]{3,2,1,0:T(8,128)(2,1)S(1)}, u32[]{:S(2)}, u32[]{:S(2)}) collective-permute-start(bf16[2,1,192,128]{3,2,1,0:T(8,128)(2,1)S(1)} %slice_bitcast_fusion.2), channel_id=1, source_target_pairs={{0,2},{2,0},{4,6},{6,4},{8,10},{10,8},{12,14},{14,12},{16,18},{18,... | collective-permute-start | bytes 294920 | tf_op jit(solution)/shard_map/ppermute | solution.py:466
  90.3 16.2 %collective-permute-start.37 = (bf16[192,1792]{1,0:T(8,128)(2,1)}, bf16[192,1792]{1,0:T(8,128)(2,1)}, u32[]{:S(2)}, u32[]{:S(2)}) collective-permute-start(bf16[192,1792]{1,0:T(8,128)(2,1)} %collective-permute-done.35.refs_5_), channel_id=1, source_target_pairs={{0,2},{2,0},{4,6},{6,4},{8,10},{10,8},{12,14},{14,12},{16,18},{18,... | collective-permute-start | bytes 2064392 | tf_op jit(solution)/shard_map/ppermute | solution.py:466
  91.6 14.1 %copy-start.6 = (bf16[1,2,2,2,192,128]{5,4,3,2,1,0:T(8,128)(2,1)}, bf16[1,2,2,2,192,128]{5,4,3,2,1,0:T(8,128)(2,1)S(1)}, u32[]{:S(2)}) copy-start(bf16[1,2,2,2,192,128]{5,4,3,2,1,0:T(8,128)(2,1)S(1)} %get-tuple-element.103) | copy-start | bytes 1179652
  91.7 20.2 %collective-permute-start.9 = (bf16[192,1792]{1,0:T(8,128)(2,1)}, bf16[192,1792]{1,0:T(8,128)(2,1)}, u32[]{:S(2)}, u32[]{:S(2)}) collective-permute-start(bf16[192,1792]{1,0:T(8,128)(2,1)} %collective-permute-done.other_ref.refs_4_), channel_id=1, source_target_pairs={{0,2},{2,0},{4,6},{6,4},{8,10},{10,8},{12,14},{14,12},{16,18},{18,... | collective-permute-start | bytes 2064392 | tf_op jit(solution)/shard_map/ppermute | solution.py:466
  92.7 9.3 %copy-start.11 = (bf16[2,1,192,128]{3,2,0,1:T(8,128)(2,1)}, bf16[2,1,192,128]{3,2,0,1:T(8,128)(2,1)S(1)}, u32[]{:S(2)}) copy-start(bf16[2,1,192,128]{3,2,0,1:T(8,128)(2,1)S(1)} %collective-permute-done.27) | copy-start | bytes 294916
  92.7 19.4 %collective-permute-start.10 = (bf16[192,1792]{1,0:T(8,128)(2,1)}, bf16[192,1792]{1,0:T(8,128)(2,1)}, u32[]{:S(2)}, u32[]{:S(2)}) collective-permute-start(bf16[192,1792]{1,0:T(8,128)(2,1)} %collective-permute-done.8.refs_5_), channel_id=1, source_target_pairs={{0,2},{2,0},{4,6},{6,4},{8,10},{10,8},{12,14},{14,12},{16,18},{18,... | collective-permute-start | bytes 2064392 | tf_op jit(solution)/shard_map/ppermute | solution.py:466
  92.8 9.1 %copy-start.12 = (bf16[2,1,192,128]{3,2,1,0:T(8,128)(2,1)}, bf16[2,1,192,128]{3,2,1,0:T(8,128)(2,1)S(1)}, u32[]{:S(2)}) copy-start(bf16[2,1,192,128]{3,2,1,0:T(8,128)(2,1)S(1)} %collective-permute-done.28.refs_3_) | copy-start | bytes 294916
  92.8 18.0 %collective-permute-start.5 = (bf16[2,2,2,192,128]{4,3,2,1,0:T(8,128)(2,1)S(1)}, bf16[2,2,2,192,128]{4,3,2,1,0:T(8,128)(2,1)}, u32[]{:S(2)}, u32[]{:S(2)}) collective-permute-start(bf16[2,2,2,192,128]{4,3,2,1,0:T(8,128)(2,1)S(1)} %get-tuple-element.102), channel_id=1, source_target_pairs={{0,8},{2,10},{4,12},{6,14},{8,0},{10,2},{12,4},{14,6},{16,24},{18,... | collective-permute-start | bytes 1179656 | tf_op jit(solution)/shard_map/ppermute | solution.py:466
  101.9 4.5 %copy-start.8 = (bf16[192,1792]{1,0:T(8,128)(2,1)S(1)}, bf16[192,1792]{1,0:T(8,128)(2,1)}, u32[]{:S(2)}) copy-start(bf16[192,1792]{1,0:T(8,128)(2,1)} %refs_4_.2) | copy-start | bytes 2064388
  105.7 13.7 %copy-start.18 = (bf16[64,1792]{1,0:T(8,128)(2,1)S(1)}, bf16[64,1792]{1,0:T(8,128)(2,1)}, u32[]{:S(2)}) copy-start(bf16[64,1792]{1,0:T(8,128)(2,1)} %get-tuple-element.87) | copy-start | bytes 688132
  105.7 14.4 %copy-start.10 = (bf16[192,1792]{1,0:T(8,128)(2,1)S(1)}, bf16[192,1792]{1,0:T(8,128)(2,1)}, u32[]{:S(2)}) copy-start(bf16[192,1792]{1,0:T(8,128)(2,1)} %input_other.1) | copy-start | bytes 2064388
  106.5 4.4 %copy-start.25 = (bf16[64,1792]{1,0:T(8,128)(2,1)S(1)}, bf16[64,1792]{1,0:T(8,128)(2,1)}, u32[]{:S(2)}) copy-start(bf16[64,1792]{1,0:T(8,128)(2,1)} %get-tuple-element.88) | copy-start | bytes 688132
  106.5 24.0 %collective-permute-start.18 = (bf16[192,1792]{1,0:T(8,128)(2,1)S(1)}, bf16[192,1792]{1,0:T(8,128)(2,1)}, u32[]{:S(2)}, u32[]{:S(2)}) collective-permute-start(bf16[192,1792]{1,0:T(8,128)(2,1)S(1)} %copy-done.8), channel_id=1, source_target_pairs={{0,2},{2,0},{4,6},{6,4},{8,10},{10,8},{12,14},{14,12},{16,18},{18,... | collective-permute-start | bytes 2064392 | tf_op jit(solution)/shard_map/ppermute | solution.py:466
  106.6 25.5 %collective-permute-start.19 = (bf16[192,1792]{1,0:T(8,128)(2,1)}, bf16[192,1792]{1,0:T(8,128)(2,1)}, u32[]{:S(2)}, u32[]{:S(2)}) collective-permute-start(bf16[192,1792]{1,0:T(8,128)(2,1)} %copy-done.24), channel_id=1, source_target_pairs={{0,2},{2,0},{4,6},{6,4},{8,10},{10,8},{12,14},{14,12},{16,18},{18,... | collective-permute-start | bytes 2064392 | tf_op jit(solution)/shard_map/ppermute | solution.py:466
  110.9 8.5 %collective-permute-start.33 = (bf16[64,1792]{1,0:T(8,128)(2,1)S(1)}, bf16[64,1792]{1,0:T(8,128)(2,1)S(1)}, u32[]{:S(2)}, u32[]{:S(2)}) collective-permute-start(bf16[64,1792]{1,0:T(8,128)(2,1)S(1)} %copy-done.25), channel_id=1, source_target_pairs={{0,4},{2,6},{4,0},{6,2},{8,12},{10,14},{12,8},{14,10},{16,20},{18,... | collective-permute-start | bytes 688136 | tf_op jit(solution)/shard_map/ppermute | solution.py:466
  111.9 8.3 %collective-permute-start.6 = (bf16[2,2,192,128]{3,2,1,0:T(8,128)(2,1)}, bf16[2,2,192,128]{3,2,1,0:T(8,128)(2,1)S(1)}, u32[]{:S(2)}, u32[]{:S(2)}) collective-permute-start(bf16[2,2,192,128]{3,2,1,0:T(8,128)(2,1)} %slice_bitcast_fusion.1), channel_id=1, source_target_pairs={{0,2},{2,0},{4,6},{6,4},{8,10},{10,8},{12,14},{14,12},{16,18},{18,... | collective-permute-start | bytes 589832 | tf_op jit(solution)/shard_map/ppermute | solution.py:466
  112.0 15.6 %collective-permute-start.39 = (bf16[64,1792]{1,0:T(8,128)(2,1)}, bf16[64,1792]{1,0:T(8,128)(2,1)S(1)}, u32[]{:S(2)}, u32[]{:S(2)}) collective-permute-start(bf16[64,1792]{1,0:T(8,128)(2,1)} %get-tuple-element.92), channel_id=1, source_target_pairs={{0,4},{2,6},{4,0},{6,2},{8,12},{10,14},{12,8},{14,10},{16,20},{18,... | collective-permute-start | bytes 688136 | tf_op jit(solution)/shard_map/ppermute | solution.py:466
  119.4 2.7 %collective-permute-start.7 = (bf16[2,2,192,128]{3,2,1,0:T(8,128)(2,1)S(1)}, bf16[2,2,192,128]{3,2,1,0:T(8,128)(2,1)S(1)}, u32[]{:S(2)}, u32[]{:S(2)}) collective-permute-start(bf16[2,2,192,128]{3,2,1,0:T(8,128)(2,1)S(1)} %slice_bitcast_fusion), channel_id=1, source_target_pairs={{0,2},{2,0},{4,6},{6,4},{8,10},{10,8},{12,14},{14,12},{16,18},{18,... | collective-permute-start | bytes 589832 | tf_op jit(solution)/shard_map/ppermute | solution.py:466
  120.1 9.6 %copy-start.16 = (bf16[64,1792]{1,0:T(8,128)(2,1)S(1)}, bf16[64,1792]{1,0:T(8,128)(2,1)}, u32[]{:S(2)}) copy-start(bf16[64,1792]{1,0:T(8,128)(2,1)} %get-tuple-element.91) | copy-start | bytes 688132
  120.2 2.7 %copy-start.26 = (bf16[2,2,192,128]{3,2,1,0:T(8,128)(2,1)}, bf16[2,2,192,128]{3,2,1,0:T(8,128)(2,1)S(1)}, u32[]{:S(2)}) copy-start(bf16[2,2,192,128]{3,2,1,0:T(8,128)(2,1)S(1)} %collective-permute-done.6.refs_2_) | copy-start | bytes 589828
  120.2 34.9 %collective-permute-start.2 = (bf16[192,1792]{1,0:T(8,128)(2,1)S(1)}, bf16[192,1792]{1,0:T(8,128)(2,1)S(1)}, u32[]{:S(2)}, u32[]{:S(2)}) collective-permute-start(bf16[192,1792]{1,0:T(8,128)(2,1)S(1)} %copy-done.10), channel_id=1, source_target_pairs={{0,1},{1,0},{2,3},{3,2},{4,5},{5,4},{6,7},{7,6},{8,9},{9,8},{10,11... | collective-permute-start | bytes 2064392 | tf_op jit(solution)/shard_map/ppermute | solution.py:462
  122.8 33.9 %collective-permute-start.32 = (bf16[64,1792]{1,0:T(8,128)(2,1)}, bf16[64,1792]{1,0:T(8,128)(2,1)S(1)}, u32[]{:S(2)}, u32[]{:S(2)}) collective-permute-start(bf16[64,1792]{1,0:T(8,128)(2,1)} %get-tuple-element.86), channel_id=1, source_target_pairs={{0,4},{2,6},{4,0},{6,2},{8,12},{10,14},{12,8},{14,10},{16,20},{18,... | collective-permute-start | bytes 688136 | tf_op jit(solution)/shard_map/ppermute | solution.py:466
  127.6 10.5 %collective-permute-start.12 = (bf16[64,1792]{1,0:T(8,128)(2,1)}, bf16[64,1792]{1,0:T(8,128)(2,1)S(1)}, u32[]{:S(2)}, u32[]{:S(2)}) collective-permute-start(bf16[64,1792]{1,0:T(8,128)(2,1)} %get-tuple-element.70), channel_id=1, source_target_pairs={{0,4},{2,6},{4,0},{6,2},{8,12},{10,14},{12,8},{14,10},{16,20},{18,... | collective-permute-start | bytes 688136 | tf_op jit(solution)/shard_map/ppermute | solution.py:466
  130.5 27.2 %collective-permute-start.34 = (bf16[64,1792]{1,0:T(8,128)(2,1)}, bf16[64,1792]{1,0:T(8,128)(2,1)S(1)}, u32[]{:S(2)}, u32[]{:S(2)}) collective-permute-start(bf16[64,1792]{1,0:T(8,128)(2,1)} %add_convert_fusion.2), channel_id=1, source_target_pairs={{0,16},{2,18},{4,20},{6,22},{8,24},{10,26},{12,28},{14,30},{16,0},... | collective-permute-start | bytes 688136 | tf_op jit(solution)/shard_map/ppermute | solution.py:466
  132.1 55.4 %copy-start = (f32[192,1792]{1,0:T(8,128)S(1)}, f32[192,1792]{1,0:T(8,128)}, u32[]{:S(2)}) copy-start(f32[192,1792]{1,0:T(8,128)} %input_own.1) | copy-start | bytes 4128772
  132.1 32.1 %collective-permute-start.38 = (bf16[64,1792]{1,0:T(8,128)(2,1)}, bf16[64,1792]{1,0:T(8,128)(2,1)}, u32[]{:S(2)}, u32[]{:S(2)}) collective-permute-start(bf16[64,1792]{1,0:T(8,128)(2,1)} %get-tuple-element.90), channel_id=1, source_target_pairs={{0,4},{2,6},{4,0},{6,2},{8,12},{10,14},{12,8},{14,10},{16,20},{18,... | collective-permute-start | bytes 688136 | tf_op jit(solution)/shard_map/ppermute | solution.py:466
  138.1 7.4 %collective-permute-start.15 = (bf16[64,1792]{1,0:T(8,128)(2,1)}, bf16[64,1792]{1,0:T(8,128)(2,1)S(1)}, u32[]{:S(2)}, u32[]{:S(2)}) collective-permute-start(bf16[64,1792]{1,0:T(8,128)(2,1)} %get-tuple-element.74), channel_id=1, source_target_pairs={{0,4},{2,6},{4,0},{6,2},{8,12},{10,14},{12,8},{14,10},{16,20},{18,... | collective-permute-start | bytes 688136 | tf_op jit(solution)/shard_map/ppermute | solution.py:466
  145.5 6.8 %collective-permute-start.21 = (bf16[64,1792]{1,0:T(8,128)(2,1)}, bf16[64,1792]{1,0:T(8,128)(2,1)S(1)}, u32[]{:S(2)}, u32[]{:S(2)}) collective-permute-start(bf16[64,1792]{1,0:T(8,128)(2,1)} %get-tuple-element.78), channel_id=1, source_target_pairs={{0,4},{2,6},{4,0},{6,2},{8,12},{10,14},{12,8},{14,10},{16,20},{18,... | collective-permute-start | bytes 688136 | tf_op jit(solution)/shard_map/ppermute | solution.py:466
  152.3 7.7 %collective-permute-start.24 = (bf16[64,1792]{1,0:T(8,128)(2,1)}, bf16[64,1792]{1,0:T(8,128)(2,1)S(1)}, u32[]{:S(2)}, u32[]{:S(2)}) collective-permute-start(bf16[64,1792]{1,0:T(8,128)(2,1)} %get-tuple-element.82), channel_id=1, source_target_pairs={{0,4},{2,6},{4,0},{6,2},{8,12},{10,14},{12,8},{14,10},{16,20},{18,... | collective-permute-start | bytes 688136 | tf_op jit(solution)/shard_map/ppermute | solution.py:466
  155.0 17.0 %collective-permute-start.40 = (bf16[64,1792]{1,0:T(8,128)(2,1)}, bf16[64,1792]{1,0:T(8,128)(2,1)S(1)}, u32[]{:S(2)}, u32[]{:S(2)}) collective-permute-start(bf16[64,1792]{1,0:T(8,128)(2,1)} %add_convert_fusion.1), channel_id=1, source_target_pairs={{0,16},{2,18},{4,20},{6,22},{8,24},{10,26},{12,28},{14,30},{16,0},... | collective-permute-start | bytes 688136 | tf_op jit(solution)/shard_map/ppermute | solution.py:466
  156.7 31.7 %copy-start.14 = (bf16[64,1792]{1,0:T(8,128)(2,1)}, bf16[64,1792]{1,0:T(8,128)(2,1)S(1)}, u32[]{:S(2)}) copy-start(bf16[64,1792]{1,0:T(8,128)(2,1)S(1)} %collective-permute-done.32.refs_1_) | copy-start | bytes 688132
  156.7 16.4 %collective-permute-start.20 = (bf16[64,1792]{1,0:T(8,128)(2,1)}, bf16[64,1792]{1,0:T(8,128)(2,1)S(1)}, u32[]{:S(2)}, u32[]{:S(2)}) collective-permute-start(bf16[64,1792]{1,0:T(8,128)(2,1)} %get-tuple-element.76), channel_id=1, source_target_pairs={{0,4},{2,6},{4,0},{6,2},{8,12},{10,14},{12,8},{14,10},{16,20},{18,... | collective-permute-start | bytes 688136 | tf_op jit(solution)/shard_map/ppermute | solution.py:466
  157.7 30.7 %copy-start.15 = (bf16[64,1792]{1,0:T(8,128)(2,1)}, bf16[64,1792]{1,0:T(8,128)(2,1)S(1)}, u32[]{:S(2)}) copy-start(bf16[64,1792]{1,0:T(8,128)(2,1)S(1)} %collective-permute-done.34.refs_2_) | copy-start | bytes 688132
  157.7 15.4 %collective-permute-start.23 = (bf16[64,1792]{1,0:T(8,128)(2,1)}, bf16[64,1792]{1,0:T(8,128)(2,1)S(1)}, u32[]{:S(2)}, u32[]{:S(2)}) collective-permute-start(bf16[64,1792]{1,0:T(8,128)(2,1)} %get-tuple-element.80), channel_id=1, source_target_pairs={{0,4},{2,6},{4,0},{6,2},{8,12},{10,14},{12,8},{14,10},{16,20},{18,... | collective-permute-start | bytes 688136 | tf_op jit(solution)/shard_map/ppermute | solution.py:466
  160.0 26.8 %collective-permute-start.22 = (bf16[64,1792]{1,0:T(8,128)(2,1)S(1)}, bf16[64,1792]{1,0:T(8,128)(2,1)S(1)}, u32[]{:S(2)}, u32[]{:S(2)}) collective-permute-start(bf16[64,1792]{1,0:T(8,128)(2,1)S(1)} %add_convert_fusion.4), channel_id=1, source_target_pairs={{0,16},{2,18},{4,20},{6,22},{8,24},{10,26},{12,28},{14,30},{16,0},... | collective-permute-start | bytes 688136 | tf_op jit(solution)/shard_map/ppermute | solution.py:466
  164.2 45.8 %collective-permute-start.11 = (bf16[64,1792]{1,0:T(8,128)(2,1)}, bf16[64,1792]{1,0:T(8,128)(2,1)S(1)}, u32[]{:S(2)}, u32[]{:S(2)}) collective-permute-start(bf16[64,1792]{1,0:T(8,128)(2,1)} %get-tuple-element.68), channel_id=1, source_target_pairs={{0,4},{2,6},{4,0},{6,2},{8,12},{10,14},{12,8},{14,10},{16,20},{18,... | collective-permute-start | bytes 688136 | tf_op jit(solution)/shard_map/ppermute | solution.py:466
  172.0 16.4 %copy-start.17 = (bf16[64,1792]{1,0:T(8,128)(2,1)}, bf16[64,1792]{1,0:T(8,128)(2,1)S(1)}, u32[]{:S(2)}) copy-start(bf16[64,1792]{1,0:T(8,128)(2,1)S(1)} %collective-permute-done.40.refs_5_) | copy-start | bytes 688132
  172.0 37.9 %collective-permute-start.14 = (bf16[64,1792]{1,0:T(8,128)(2,1)}, bf16[64,1792]{1,0:T(8,128)(2,1)}, u32[]{:S(2)}, u32[]{:S(2)}) collective-permute-start(bf16[64,1792]{1,0:T(8,128)(2,1)} %get-tuple-element.72), channel_id=1, source_target_pairs={{0,4},{2,6},{4,0},{6,2},{8,12},{10,14},{12,8},{14,10},{16,20},{18,... | collective-permute-start | bytes 688136 | tf_op jit(solution)/shard_map/ppermute | solution.py:466
  173.1 13.7 %copy-start.21 = (bf16[64,1792]{1,0:T(8,128)(2,1)}, bf16[64,1792]{1,0:T(8,128)(2,1)S(1)}, u32[]{:S(2)}) copy-start(bf16[64,1792]{1,0:T(8,128)(2,1)S(1)} %collective-permute-done.20.refs_1_) | copy-start | bytes 688132
  173.1 36.9 %collective-permute-start.13 = (bf16[64,1792]{1,0:T(8,128)(2,1)S(1)}, bf16[64,1792]{1,0:T(8,128)(2,1)}, u32[]{:S(2)}, u32[]{:S(2)}) collective-permute-start(bf16[64,1792]{1,0:T(8,128)(2,1)S(1)} %add_convert_fusion.6), channel_id=1, source_target_pairs={{0,16},{2,18},{4,20},{6,22},{8,24},{10,26},{12,28},{14,30},{16,0},... | collective-permute-start | bytes 688136 | tf_op jit(solution)/shard_map/ppermute | solution.py:466
  173.1 13.7 %copy-start.22 = (bf16[64,1792]{1,0:T(8,128)(2,1)}, bf16[64,1792]{1,0:T(8,128)(2,1)S(1)}, u32[]{:S(2)}) copy-start(bf16[64,1792]{1,0:T(8,128)(2,1)S(1)} %collective-permute-done.23.refs_4_) | copy-start | bytes 688132
  173.1 36.9 %collective-permute-start.16 = (bf16[64,1792]{1,0:T(8,128)(2,1)}, bf16[64,1792]{1,0:T(8,128)(2,1)}, u32[]{:S(2)}, u32[]{:S(2)}) collective-permute-start(bf16[64,1792]{1,0:T(8,128)(2,1)} %add_convert_fusion.5), channel_id=1, source_target_pairs={{0,16},{2,18},{4,20},{6,22},{8,24},{10,26},{12,28},{14,30},{16,0},... | collective-permute-start | bytes 688136 | tf_op jit(solution)/shard_map/ppermute | solution.py:466
  187.5 18.5 %collective-permute-start.25 = (bf16[64,1792]{1,0:T(8,128)(2,1)S(1)}, bf16[64,1792]{1,0:T(8,128)(2,1)}, u32[]{:S(2)}, u32[]{:S(2)}) collective-permute-start(bf16[64,1792]{1,0:T(8,128)(2,1)S(1)} %add_convert_fusion.3), channel_id=1, source_target_pairs={{0,16},{2,18},{4,20},{6,22},{8,24},{10,26},{12,28},{14,30},{16,0},... | collective-permute-start | bytes 688136 | tf_op jit(solution)/shard_map/ppermute | solution.py:466
  (5 other events, 3.9 us)
where the time goes:
time: 215 us
  waiting for transfers between devices  79.6 us (37%)
  Pallas kernels  71 us (33%)
  starting transfers between devices  48 us (22%)
  other arithmetic  8.48 us (4%)
  local copies, waits for them, and re-layouts  5.86 us (3%)
    ppermute x36, waiting for transfers between devices, over(): return lax.ppermute(v, 'dp', pairs)  63.9 us
    ppermute x36, starting transfers between devices, over(): return lax.ppermute(v, 'dp', pairs)  40.6 us
    pallas_call x4, Pallas kernels, weight_grad(): pl.pallas_call(body, out_shape=(out,) * (kinds * owners), grid_spec=pltpu...  17.2 us
    ppermute x5, waiting for transfers between devices, over_y(): lax.ppermute(v, 'tp', [(i, (i + 1) % tp_size) for i in range(tp_size)])  15.8 us
    pallas_call x2, Pallas kernels, input_part(): pl.pallas_call(body, out_shape=jax.ShapeDtypeStruct((rows, half), jnp.bfl...  14.6 us
    pallas_call x3, Pallas kernels, adam(): pl.pallas_call(body, out_shape=(jax.ShapeDtypeStruct(master.shape, jnp.fl...  11.9 us
    pallas_call x1, Pallas kernels, own_part(): pl.pallas_call(body, out_shape=(out,) * 3, grid_spec=pltpu.PrefetchScalar...  10.2 us
    pallas_call x1, Pallas kernels, gate_up(): pl.pallas_call(body, out_shape=(out, out, *shapes), grid_spec=pltpu.Prefe...  9.31 us
  transfers between devices with their start and end apart: 41, of which 10 were waited for; matrix products, arithmetic and copies ran while one was open for 5% of the time, Pallas kernels for 31%

commit v1 on v0

--- a/solution.py
+++ b/solution.py
@@ -176,6 +176,7 @@
         cost_estimate=pl.CostEstimate(
             flops=6 * rows * half * steps * WIDE, bytes_accessed=6 * half * steps * WIDE, transcendentals=0
         ),
+        compiler_params=pltpu.CompilerParams(vmem_limit_bytes=34 << 20),
         name="own_part",
     )(scalars, tokens, cotangent, *[working] * 3)
 
@@ -252,6 +253,7 @@
             bytes_accessed=4 * half * steps * WIDE + 16 * rows * steps * WIDE,
             transcendentals=rows * steps * WIDE,
         ),
+        compiler_params=pltpu.CompilerParams(vmem_limit_bytes=28 << 20),
         name="gate_up",
     )(scalars, other, *[working] * 2, gate, up)
 
@@ -290,6 +292,7 @@
             bytes_accessed=2 * half * steps * WIDE + 20 * rows * steps * WIDE,
             transcendentals=0,
         ),
+        compiler_params=pltpu.CompilerParams(vmem_limit_bytes=20 << 20),
         name="down_acts",
     )(scalars, other, working, partial, act, slope)
 
@@ -330,6 +333,7 @@
         cost_estimate=pl.CostEstimate(
             flops=4 * rows * half * steps * WIDE, bytes_accessed=4 * half * steps * WIDE, transcendentals=0
         ),
+        compiler_params=pltpu.CompilerParams(vmem_limit_bytes=24 << 20),
         name="input_other" if side else "input_own",
     )(scalars, grads, *[working] * 2)
 
@@ -344,8 +348,8 @@
     tile = half // 2 if half % (2 * BLOCK) == 0 else half
 
     def body(s, *refs):
-        a_refs, x_refs, outs = refs[:group], refs[group : 2 * group], refs[2 * group : 2 * group + kinds * owners]
-        left, value = refs[2 * group + kinds * owners :]
+        a_refs, x_refs, outs = refs[:group], refs[group : 2 * group], refs[2 * group : -2]
+        left, value = refs[-2:]
 
         @pl.when(pl.program_id(0) == 0)
         def _():
@@ -361,7 +365,11 @@
             value[...] = dot32(left[kind], right, contract_mid).astype(jnp.bfloat16)
             for relation in range(owners):
                 start = pl.multiple_of(jnp.bitwise_xor(s[0], relation) * narrow, narrow)
-                outs[kind * owners + relation][...] = value[pl.ds(start, narrow), :]
+                piece = value[pl.ds(start, narrow), :]
+                if relation == 1:
+                    outs[-1][kind * narrow : (kind + 1) * narrow, :] = piece
+                else:
+                    outs[kind * (owners - 1) + max(relation - 1, 0)][...] = piece
 
     def act_spec(a):
         if a.ndim == 5:
@@ -371,12 +379,14 @@
     out = jax.ShapeDtypeStruct((narrow, half), jnp.bfloat16)
     made = pl.pallas_call(
         body,
-        out_shape=(out,) * (kinds * owners),
+        out_shape=(out,) * (kinds * (owners - 1))
+        + (jax.ShapeDtypeStruct((kinds * narrow, half), jnp.bfloat16),),
         grid_spec=pltpu.PrefetchScalarGridSpec(
             num_scalar_prefetch=1,
             grid=(half // tile,),
             in_specs=[act_spec(a) for a in acts] + [pl.BlockSpec((rows, tile), lambda i, s: (0, i))] * group,
-            out_specs=(pl.BlockSpec((narrow, tile), lambda i, s: (0, i)),) * (kinds * owners),
+            out_specs=(pl.BlockSpec((narrow, tile), lambda i, s: (0, i)),) * (kinds * (owners - 1))
+            + (pl.BlockSpec((kinds * narrow, tile), lambda i, s: (0, i)),),
             scratch_shapes=[
                 pltpu.VMEM((kinds, wide, group * rows), jnp.bfloat16),
                 pltpu.VMEM((wide, tile), jnp.bfloat16),
@@ -387,19 +397,25 @@
             bytes_accessed=2 * group * rows * half + 2 * kinds * wide * half,
             transcendentals=0,
         ),
+        compiler_params=pltpu.CompilerParams(vmem_limit_bytes=20 << 20),
     )(own, *acts, *inputs)
-    return [made[kind * owners : (kind + 1) * owners] for kind in range(kinds)]
-
-
-def adam(me, sums, kinds, halves, master, moment_one, moment_two, before, replicas):
-    rows, half = sums[0][0].shape
+    return [made[kind * (owners - 1) : (kind + 1) * (owners - 1)] for kind in range(kinds)], made[-1]
+
+
+def adam(me, sums, pieces, master, moment_one, moment_two, before, replicas):
+    rows, half = sums[0][0][0].shape
     count = len(sums[0])
     steps = len(sums)
     columns = master.shape[2] // half
 
+    def pick(values, i):
+        chosen = values[0]
+        for at in range(1, steps):
+            chosen = jnp.where(i == at, values[at], chosen)
+        return chosen
+
     def at(i, s):
-        kind = kinds[0] + i * (kinds[1] - kinds[0])
-        return (kind, 0, (s[0] + halves[0] + i * (halves[1] - halves[0])) % columns)
+        return (pick([p[0] for p in pieces], i), 0, (s[0] + pick([p[1] for p in pieces], i)) % columns)
 
     state = pl.BlockSpec((1, rows, half), at)
 
@@ -430,7 +446,7 @@
         grid_spec=pltpu.PrefetchScalarGridSpec(
             num_scalar_prefetch=1,
             grid=(steps,),
-            in_specs=[pl.BlockSpec((rows, half), lambda i, s: (0, 0))] * len(flat)
+            in_specs=[pl.BlockSpec((rows, half), lambda i, s, row=row: (row, 0)) for _, row in flat]
             + [state] * 3
             + [pl.BlockSpec(memory_space=pl.ANY)] * len(extra),
             out_specs=(state,) * 3,
@@ -439,8 +455,9 @@
         cost_estimate=pl.CostEstimate(
             flops=20 * steps * rows * half, bytes_accessed=28 * steps * rows * half, transcendentals=0
         ),
+        compiler_params=pltpu.CompilerParams(vmem_limit_bytes=16 << 20),
         name="adam",
-    )(me, *flat, master, moment_one, moment_two, *extra)
+    )(me, *[part for part, _ in flat], master, moment_one, moment_two, *extra)
 
 
 def grouped(*args):
@@ -493,6 +510,7 @@
     c_other, h_theirs = after((c_other, h_theirs))
     h_from = over_y(h_theirs)
     c_other_s = over_s(c_other)
+    t_other_s = over_s(t_other)
     grads, d_theirs, d_mine = down_acts(scalars, c_other, working, down, act, slope, layout)
     h_from, d_theirs = after((h_from, d_theirs))
     d_from = over_y(d_theirs)
@@ -504,7 +522,6 @@
         return [near, near_s, over_core(near[1]), over_core(near_s[1])]
 
     hidden_acts = spread(h_mine, h_from)
-    t_other_s = over_s(t_other)
     c_acts = [
         [c_own, c_own_s, c_own_c, over_core(c_own_s)], [c_other, c_other_s, over_core(c_other), over_core(c_other_s)]
     ]
@@ -513,24 +530,21 @@
     ]
     grad_acts = spread(d_mine, d_from)
 
-    made = []
-    for h in range(2):
-        made += weight_grad(hidden_acts, c_acts[h], own)
-    for h in range(2):
-        made += weight_grad(grad_acts, t_acts[h], own)
     sums = []
-    for keep, far_x, far_z, far_both in made:
-        came = over_x(far_both)
-        far_z = (far_z.astype(jnp.float32) + came.astype(jnp.float32)).astype(jnp.bfloat16)
-        sums.append((keep, over_x(far_x), over_m(far_z)))
+    for call in range(4):
+        acts, inputs = (hidden_acts, c_acts[call]) if call < 2 else (grad_acts, t_acts[call - 2])
+        made, far_x = weight_grad(acts, inputs, own)
+        side = over_x(far_x)
+        for row, (keep, far_z, far_both) in enumerate(made):
+            came = over_x(far_both)
+            far_z = (far_z.astype(jnp.float32) + came.astype(jnp.float32)).astype(jnp.bfloat16)
+            sums.append(((keep, 0), (side, row), (over_m(far_z), 0)))
     state = None
-    for at in range(0, len(PIECES), 2):
-        kinds, halves = zip(*PIECES[at : at + 2])
+    for low, high in ((0, 4), (4, 6)):
         state = adam(
             me.astype(jnp.int32).reshape(1),
-            sums[at : at + 2],
-            kinds,
-            halves,
+            sums[low:high],
+            PIECES[low:high],
             master,
             moment_one,
             moment_two,

time: 215 us -> 204 us (0.949)
  waiting for transfers between devices: 79.6 us -> 101 us
  Pallas kernels: 71 us -> 49.7 us
  starting transfers between devices: 48 us -> 40.2 us
  other arithmetic: 8.48 us -> 2.46 us
  local copies, waits for them, and re-layouts: 5.86 us -> 8.95 us
    ppermute x36 -> x34, waiting for transfers between devices: 63.9 us -> 85.3 us  [over(): return lax.ppermute(v, 'dp', pairs)]
    ppermute x36 -> x34, starting transfers between devices: 40.6 us -> 32.9 us  [over(): return lax.ppermute(v, 'dp', pairs)]
    pallas_call x4, Pallas kernels: 17.2 us -> 11.2 us  [weight_grad(): pl.pallas_call(body, out_shape=(out,) * (kinds * (owners - 1)) + (jax.Sha...]
    convert_element_type x6, other arithmetic: 6.29 us -> 0.33 us  [grouped_step(): (far_z.astype(jnp.float32) + came.astype(jnp.float32)).astype(jnp.bfloat16)]
    pallas_call x3 -> x2, Pallas kernels: 11.9 us -> 6.44 us  [adam(): pl.pallas_call(body, out_shape=(jax.ShapeDtypeStruct(master.shape, jnp.fl...]
    unnamed x56 -> x28, local copies, waits for them, and re-layouts: 2.9 us -> 8.18 us
    pallas_call x1, Pallas kernels: 7.78 us -> 4.91 us  [down_acts(): pl.pallas_call(body, out_shape=(jax.ShapeDtypeStruct((steps, 2, rows, WID...]
    pallas_call x2, Pallas kernels: 14.6 us -> 11.8 us  [input_part(): pl.pallas_call(body, out_shape=jax.ShapeDtypeStruct((rows, half), jnp.bfl...]
  transfers between devices with their start and end apart: 41 -> 39, of which waited for: 10 -> 12; matrix products, arithmetic and copies ran while one was open for 5% -> 2% of each run, Pallas kernels for 31% -> 23%
where the time goes in v1:
time: 204 us
  waiting for transfers between devices  101 us (50%)
  Pallas kernels  49.7 us (24%)
  starting transfers between devices  40.2 us (20%)
  local copies, waits for them, and re-layouts  8.95 us (4%)
  other arithmetic  2.46 us (1%)
    ppermute x34, waiting for transfers between devices, over(): return lax.ppermute(v, 'dp', pairs)  85.3 us
    ppermute x34, starting transfers between devices, over(): return lax.ppermute(v, 'dp', pairs)  32.9 us
    ppermute x5, waiting for transfers between devices, over_y(): lax.ppermute(v, 'tp', [(i, (i + 1) % tp_size) for i in range(tp_size)])  15.7 us
    pallas_call x2, Pallas kernels, input_part(): pl.pallas_call(body, out_shape=jax.ShapeDtypeStruct((rows, half), jnp.bfl...  11.8 us
    pallas_call x4, Pallas kernels, weight_grad(): pl.pallas_call(body, out_shape=(out,) * (kinds * (owners - 1)) + (jax.Sha...  11.2 us
    unnamed x28, local copies, waits for them, and re-layouts  8.18 us
    pallas_call x1, Pallas kernels, own_part(): pl.pallas_call(body, out_shape=(out,) * 3, grid_spec=pltpu.PrefetchScalar...  7.76 us
    pallas_call x1, Pallas kernels, gate_up(): pl.pallas_call(body, out_shape=(out, out, *shapes), grid_spec=pltpu.Prefe...  7.6 us
  transfers between devices with their start and end apart: 39, of which 12 were waited for; matrix products, arithmetic and copies ran while one was open for 2% of the time, Pallas kernels for 23%

profile of v1, /device:TPU:0, one launch (start us, length us, event | category | flops | bytes accessed | tf_op | source)
XLA Modules:
  0.0 203.9 jit_solution(13086282898812254307)
XLA Ops:
  0.6 3.1 %collective-permute-start = (bf16[192,1792]{1,0:T(8,128)(2,1)}, bf16[192,1792]{1,0:T(8,128)(2,1)S(1)}, u32[]{:S(2)}, u32[]{:S(2)}) collective-permute-start(bf16[192,1792]{1,0:T(8,128)(2,1)} %refs_4_.3), channel_id=1, source_target_pairs={{0,1},{1,0},{2,3},{3,2},{4,5},{5,4},{6,7},{7,6},{8,9},{9,8},{10,11... | collective-permute-start | bytes 2064392 | tf_op jit(solution)/shard_map/ppermute | solution.py:479
  3.7 15.6 %collective-permute-done.other_ref.refs_4_ = bf16[192,1792]{1,0:T(8,128)(2,1)S(1)} collective-permute-done((bf16[192,1792]{1,0:T(8,128)(2,1)}, bf16[192,1792]{1,0:T(8,128)(2,1)S(1)}, u32[]{:S(2)}, u32[]{:S(2)}) %collective-permute-start) | collective-permute-done | bytes 688160 | tf_op jit(solution)/shard_map/ppermute | solution.py:479
  19.3 0.8 copy-done.11
  20.2 1.7 collective-permute-start.1
  21.9 1.6 collective-permute-start.31
  23.5 0.4 collective-permute-start.19
  24.6 0.7 stack.15.s
  25.3 1.1 copy-done.3
  26.4 1.1 copy-done.9
  27.5 7.8 %own_part.1 = (f32[4,192,512]{2,1,0:T(8,128)S(1)}, f32[4,192,512]{2,1,0:T(8,128)S(1)}, f32[4,192,512]{2,1,0:T(8,128)S(1)}) custom-call(s32[5]{0:T(128)S(1)} %stack.15.s, bf16[192,1792]{1,0:T(8,128)(2,1)S(1)} %copy-done.9, bf16[192,1792]{1,0:T(8,128)(2,1)S(1)} %copy-done.3, bf16[1,1,3,2048,3584]{4,3,2,1,0:T(8,128)(2,1)} %w1.5, ...), custom_call_target="tpu_custom_call" | custom-call | flops 4227858432 | bytes 22020096 | tf_op jit(solution)/shard_map/own_part/pallas_call | solution.py:167
  35.3 7.6 %gate_up.1 = (f32[4,192,512]{2,1,0:T(8,128)S(1)}, f32[4,192,512]{2,1,0:T(8,128)S(1)}, bf16[2,2,2,1,192,128]{5,4,3,2,1,0:T(8,128)(2,1)}, bf16[2,2,2,1,192,128]{5,4,3,2,1,0:T(8,128)(2,1)S(1)}) custom-call(s32[5]{0:T(128)S(1)} %stack.15.s, bf16[192,1792]{1,0:T(8,128)(2,1)S(1)} %copy-done.12, bf16[1,1,3,2048,3584]{4,3,2,1,0:T(8,128)(2,1)} %w1.5, ...), custom_call_target="tpu_custom_call" | custom-call | flops 2818572288 | bytes 20971520 | tf_op jit(solution)/shard_map/gate_up/pallas_call | solution.py:242
  42.9 1.1 copy-done.5
  44.1 1.1 copy-done.7
  45.2 0.3 collective-permute-start.3
  45.5 4.8 %collective-permute-start.20 = (bf16[192,1792]{1,0:T(8,128)(2,1)S(1)}, bf16[192,1792]{1,0:T(8,128)(2,1)}, u32[]{:S(2)}, u32[]{:S(2)}) collective-permute-start(bf16[192,1792]{1,0:T(8,128)(2,1)S(1)} %copy-done.4), channel_id=1, source_target_pairs={{0,2},{2,0},{4,6},{6,4},{8,10},{10,8},{12,14},{14,12},{16,18},{18,... | collective-permute-start | bytes 2064392 | tf_op jit(solution)/shard_map/ppermute | solution.py:483
  50.3 3.7 %collective-permute-start.8 = (bf16[192,1792]{1,0:T(8,128)(2,1)}, bf16[192,1792]{1,0:T(8,128)(2,1)S(1)}, u32[]{:S(2)}, u32[]{:S(2)}) collective-permute-start(bf16[192,1792]{1,0:T(8,128)(2,1)} %copy-done.11), channel_id=1, source_target_pairs={{0,8},{2,10},{4,12},{6,14},{8,0},{10,2},{12,4},{14,6},{16,24},{18,... | collective-permute-start | bytes 2064392 | tf_op jit(solution)/shard_map/ppermute | solution.py:483
  53.9 1.4 copy-done.6
  55.4 1.4 copy-done.8
  56.8 4.9 %down_acts.1 = (bf16[4,2,192,512]{3,2,1,0:T(8,128)(2,1)S(1)}, bf16[2,2,2,2,192,128]{5,4,3,2,1,0:T(8,128)(2,1)S(1)}, bf16[2,2,2,2,192,128]{5,4,3,2,1,0:T(8,128)(2,1)S(1)}) custom-call(s32[5]{0:T(128)S(1)} %stack.15.s, bf16[192,1792]{1,0:T(8,128)(2,1)S(1)} %collective-permute-done.1.other_ref.refs_4_, bf16[1,1,3,2048,3584]{4,3,2,1,0:T(8,128)(2,1)} %w1.5, ...), custom_call_target="tpu_custom_call" | custom-call | flops 1409286144 | bytes 15204352 | tf_op jit(solution)/shard_map/down_acts/pallas_call | solution.py:281
  61.7 0.2 collective-permute-start.4
  61.9 1.1 fusion.1
  63.0 2.0 collective-permute-start.25
  65.0 0.1 collective-permute-start.16
  65.1 5.9 %input_other.1 = bf16[192,1792]{1,0:T(8,128)(2,1)S(1)} custom-call(s32[5]{0:T(128)S(1)} %stack.15.s, bf16[4,2,192,512]{3,2,1,0:T(8,128)(2,1)S(1)} %get-tuple-element.57.grads_ref, bf16[1,1,3,2048,3584]{4,3,2,1,0:T(8,128)(2,1)} %w1.5, bf16[1,1,3,2048,3584]{4,3,2,1,0:T(8,128)(2,1)} %w1.5), custom_call_target="tpu_custom_call" | custom-call | flops 2818572288 | bytes 14680064 | tf_op jit(solution)/shard_map/input_other/pallas_call | solution.py:322
  71.0 18.2 %collective-permute-done.16 = bf16[2,2,1,192,128]{4,3,1,2,0:T(8,128)(2,1)S(1)} collective-permute-done((bf16[2,2,1,192,128]{4,3,1,2,0:T(8,128)(2,1)S(1)}, bf16[2,2,1,192,128]{4,3,1,2,0:T(8,128)(2,1)S(1)}, u32[]{:S(2)}, u32[]{:S(2)}) %collective-permute-start.16) | collective-permute-done | bytes 196640 | tf_op jit(solution)/shard_map/ppermute | solution.py:483
  89.3 0.6 collective-permute-start.26
  89.8 0.1 collective-permute-start.17
  89.9 0.4 collective-permute-start.18
  90.3 0.1 collective-permute-start.27
  90.5 1.1 collective-permute-done.21.refs_7_
  91.6 0.1 collective-permute-start.9
  91.7 1.0 collective-permute-done.17
  92.7 0.1 collective-permute-start.10
  92.8 1.7 collective-permute-start.5
  94.6 5.9 %input_own.1 = f32[192,1792]{1,0:T(8,128)S(1)} custom-call(s32[5]{0:T(128)S(1)} %stack.15.s, bf16[4,2,192,512]{3,2,1,0:T(8,128)(2,1)S(1)} %get-tuple-element.57.grads_ref, bf16[1,1,3,2048,3584]{4,3,2,1,0:T(8,128)(2,1)} %w1.5, bf16[1,1,3,2048,3584]{4,3,2,1,0:T(8,128)(2,1)} %w1.5), custom_call_target="tpu_custom_call" | custom-call | flops 2818572288 | bytes 14680064 | tf_op jit(solution)/shard_map/input_own/pallas_call | solution.py:322
  100.5 2.7 %shard_map.112 = (bf16[64,1792]{1,0:T(8,128)(2,1)S(1)}, bf16[64,1792]{1,0:T(8,128)(2,1)S(1)}, bf16[64,1792]{1,0:T(8,128)(2,1)S(1)}, bf16[64,1792]{1,0:T(8,128)(2,1)S(1)}) custom-call(s32[1]{0:T(128)} %bitcast.4.s, bf16[2,2,1,192,128]{4,3,2,1,0:T(8,128)(2,1)S(1)} %bitcast.26, bf16[2,2,1,192,128]{4,3,2,1,0:T(8,128)(2,1)S(1)} %bitcast.28, ...), custom_call_target="tpu_custom_call" | custom-call | flops 704643072 | bytes 3670016 | tf_op jit(solution)/shard_map/pallas_call | solution.py:380
  103.4 0.5 collective-permute-start.33
  103.9 1.8 shard_map.113
  105.8 0.2 collective-permute-start.6
  105.9 2.0 collective-permute-start.29
  107.9 6.3 %collective-permute-done.23 = bf16[64,1792]{1,0:T(8,128)(2,1)S(1)} collective-permute-done((bf16[64,1792]{1,0:T(8,128)(2,1)S(1)}, bf16[64,1792]{1,0:T(8,128)(2,1)S(1)}, u32[]{:S(2)}, u32[]{:S(2)}) %collective-permute-start.23) | collective-permute-done | bytes 229408 | tf_op jit(solution)/shard_map/ppermute | solution.py:483
  114.3 1.9 collective-permute-start.2
  116.2 2.8 %shard_map.111 = (bf16[64,1792]{1,0:T(8,128)(2,1)S(1)}, bf16[64,1792]{1,0:T(8,128)(2,1)S(1)}, bf16[64,1792]{1,0:T(8,128)(2,1)S(1)}, bf16[64,1792]{1,0:T(8,128)(2...) custom-call(s32[1]{0:T(128)} %bitcast.4.s, ...), custom_call_target="tpu_custom_call" | custom-call | flops 1409286144 | bytes 4587520 | tf_op jit(solution)/shard_map/pallas_call | solution.py:380
  119.0 2.1 %collective-permute-start.12 = (bf16[64,1792]{1,0:T(8,128)(2,1)S(1)}, bf16[64,1792]{1,0:T(8,128)(2,1)S(1)}, u32[]{:S(2)}, u32[]{:S(2)}) collective-permute-start(bf16[64,1792]{1,0:T(8,128)(2,1)S(1)} %get-tuple-element.65), channel_id=1, source_target_pairs={{0,4},{2,6},{4,0},{6,2},{8,12},{10,14},{12,8},{14,10},{16,20},{18,... | collective-permute-start | bytes 688136 | tf_op jit(solution)/shard_map/ppermute | solution.py:483
  121.2 1.7 collective-permute-start.24
  122.9 1.9 collective-permute-start.28
  124.8 3.9 %shard_map.114 = (bf16[64,1792]{1,0:T(8,128)(2,1)S(1)}, bf16[64,1792]{1,0:T(8,128)(2,1)S(1)}, bf16[64,1792]{1,0:T(8,128)(2,1)S(1)}, bf16[64,1792]{1,0:T(8,128)(2...) custom-call(s32[1]{0:T(128)} %bitcast.4.s, ...), custom_call_target="tpu_custom_call" | custom-call | flops 1409286144 | bytes 4587520 | tf_op jit(solution)/shard_map/pallas_call | solution.py:380
  128.7 0.9 collective-permute-done.12
  129.7 9.0 %collective-permute-done.14 = bf16[64,1792]{1,0:T(8,128)(2,1)S(1)} collective-permute-done((bf16[64,1792]{1,0:T(8,128)(2,1)S(1)}, bf16[64,1792]{1,0:T(8,128)(2,1)S(1)}, u32[]{:S(2)}, u32[]{:S(2)}) %collective-permute-start.14) | collective-permute-done | bytes 229408 | tf_op jit(solution)/shard_map/ppermute | solution.py:483
  138.7 0.3 collective-permute-start.35
  139.0 6.5 %collective-permute-done.35 = bf16[64,1792]{1,0:T(8,128)(2,1)S(1)} collective-permute-done((bf16[64,1792]{1,0:T(8,128)(2,1)S(1)}, bf16[64,1792]{1,0:T(8,128)(2,1)S(1)}, u32[]{:S(2)}, u32[]{:S(2)}) %collective-permute-start.35) | collective-permute-done | bytes 229408 | tf_op jit(solution)/shard_map/ppermute | solution.py:483
  145.6 0.6 collective-permute-start.37
  146.2 2.9 %collective-permute-start.30 = (bf16[64,1792]{1,0:T(8,128)(2,1)S(1)}, bf16[64,1792]{1,0:T(8,128)(2,1)S(1)}, u32[]{:S(2)}, u32[]{:S(2)}) collective-permute-start(bf16[64,1792]{1,0:T(8,128)(2,1)S(1)} %add_convert_fusion.3), channel_id=1, source_target_pairs={{0,16},{2,18},{4,20},{6,22},{8,24},{10,26},{12,28},{14,30},{16,0},... | collective-permute-start | bytes 688136 | tf_op jit(solution)/shard_map/ppermute | solution.py:483
  149.0 2.5 %collective-permute-done.37 = bf16[64,1792]{1,0:T(8,128)(2,1)S(1)} collective-permute-done((bf16[64,1792]{1,0:T(8,128)(2,1)S(1)}, bf16[64,1792]{1,0:T(8,128)(2,1)S(1)}, u32[]{:S(2)}, u32[]{:S(2)}) %collective-permute-start.37) | collective-permute-done | bytes 229408 | tf_op jit(solution)/shard_map/ppermute | solution.py:483
  151.6 2.0 %collective-permute-start.36 = (bf16[64,1792]{1,0:T(8,128)(2,1)S(1)}, bf16[64,1792]{1,0:T(8,128)(2,1)S(1)}, u32[]{:S(2)}, u32[]{:S(2)}) collective-permute-start(bf16[64,1792]{1,0:T(8,128)(2,1)S(1)} %add_convert_fusion.2), channel_id=1, source_target_pairs={{0,16},{2,18},{4,20},{6,22},{8,24},{10,26},{12,28},{14,30},{16,0},... | collective-permute-start | bytes 688136 | tf_op jit(solution)/shard_map/ppermute | solution.py:483
  153.7 1.4 collective-permute-start.11
  155.1 0.7 collective-permute-start.34
  155.8 0.9 collective-permute-start.13
  156.7 12.0 %collective-permute-done.30.refs_5_ = bf16[64,1792]{1,0:T(8,128)(2,1)S(1)} collective-permute-done((bf16[64,1792]{1,0:T(8,128)(2,1)S(1)}, bf16[64,1792]{1,0:T(8,128)(2,1)S(1)}, u32[]{:S(2)}, u32[]{:S(2)}) %collective-permute-start.30) | collective-permute-done | bytes 229408 | tf_op jit(solution)/shard_map/ppermute | solution.py:483
  168.7 9.8 %collective-permute-done.36.refs_8_ = bf16[64,1792]{1,0:T(8,128)(2,1)S(1)} collective-permute-done((bf16[64,1792]{1,0:T(8,128)(2,1)S(1)}, bf16[64,1792]{1,0:T(8,128)(2,1)S(1)}, u32[]{:S(2)}, u32[]{:S(2)}) %collective-permute-start.36) | collective-permute-done | bytes 229408 | tf_op jit(solution)/shard_map/ppermute | solution.py:483
  178.5 1.0 add_convert_fusion
  179.5 17.9 %collective-permute-done.38.refs_11_ = bf16[64,1792]{1,0:T(8,128)(2,1)S(1)} collective-permute-done((bf16[64,1792]{1,0:T(8,128)(2,1)S(1)}, bf16[64,1792]{1,0:T(8,128)(2,1)S(1)}, u32[]{:S(2)}, u32[]{:S(2)}) %collective-permute-start.38) | collective-permute-done | bytes 229408 | tf_op jit(solution)/shard_map/ppermute | solution.py:483
  197.4 4.1 %adam.2 = (f32[3,64,3584]{2,1,0:T(8,128)}, f32[3,64,3584]{2,1,0:T(8,128)}, f32[3,64,3584]{2,1,0:T(8,128)}) custom-call(s32[1]{0:T(128)} %bitcast.1.s, bf16[64,1792]{1,0:T(8,128)(2,1)S(1)} %get-tuple-element.71.refs_0_, bf16[64,1792]{1,0:T(8,128)(2,1)S(1)} %collective-permute-done.22.refs_1_, bf16[64,1792]{1,0:T(8,128)(2,1)S(1)} %collective-permute-done.24.refs_2_, ...), custom_call_target="tpu_custom_call" | custom-call | flops 9175040 | bytes 12845056 | tf_op jit(solution)/shard_map/adam/pallas_call | solution.py:443
  201.5 2.4 %adam.3 = (f32[3,64,3584]{2,1,0:T(8,128)}, f32[3,64,3584]{2,1,0:T(8,128)}, f32[3,64,3584]{2,1,0:T(8,128)}) custom-call(s32[1]{0:T(128)} %bitcast.1.s, bf16[64,1792]{1,0:T(8,128)(2,1)S(1)} %get-tuple-element.62.refs_0_, bf16[128,1792]{1,0:T(8,128)(2,1)S(1)} %collective-permute-done.11.refs_1_.refs_4_, ...), custom_call_target="tpu_custom_call", output_to_operand_aliasing={{0}: (10, {}), {1}: (11, {}), {2}: (12, {})} | custom-call | flops 4587520 | bytes 6422528 | tf_op jit(solution)/shard_map/adam/pallas_call | solution.py:443
  (67 shorter events, 0.7 us)
Async XLA Ops:
  0.6 18.7 %collective-permute-start = (bf16[192,1792]{1,0:T(8,128)(2,1)}, bf16[192,1792]{1,0:T(8,128)(2,1)S(1)}, u32[]{:S(2)}, u32[]{:S(2)}) collective-permute-start(bf16[192,1792]{1,0:T(8,128)(2,1)} %refs_4_.3), channel_id=1, source_target_pairs={{0,1},{1,0},{2,3},{3,2},{4,5},{5,4},{6,7},{7,6},{8,9},{9,8},{10,11... | collective-permute-start | bytes 2064392 | tf_op jit(solution)/shard_map/ppermute | solution.py:479
  19.3 0.8 copy-start.11
  20.2 25.0 %collective-permute-start.1 = (bf16[192,1792]{1,0:T(8,128)(2,1)}, bf16[192,1792]{1,0:T(8,128)(2,1)S(1)}, u32[]{:S(2)}, u32[]{:S(2)}) collective-permute-start(bf16[192,1792]{1,0:T(8,128)(2,1)} %refs_4_.2), channel_id=1, source_target_pairs={{0,1},{1,0},{2,3},{3,2},{4,5},{5,4},{6,7},{7,6},{8,9},{9,8},{10,11... | collective-permute-start | bytes 2064392 | tf_op jit(solution)/shard_map/ppermute | solution.py:479
  21.9 41.1 %collective-permute-start.31 = (bf16[192,1792]{1,0:T(8,128)(2,1)}, bf16[192,1792]{1,0:T(8,128)(2,1)}, u32[]{:S(2)}, u32[]{:S(2)}) collective-permute-start(bf16[192,1792]{1,0:T(8,128)(2,1)} %refs_4_.3), channel_id=1, source_target_pairs={{0,8},{2,10},{4,12},{6,14},{8,0},{10,2},{12,4},{14,6},{16,24},{18,... | collective-permute-start | bytes 2064392 | tf_op jit(solution)/shard_map/ppermute | solution.py:483
  23.5 41.5 %collective-permute-start.19 = (bf16[192,1792]{1,0:T(8,128)(2,1)}, bf16[192,1792]{1,0:T(8,128)(2,1)}, u32[]{:S(2)}, u32[]{:S(2)}) collective-permute-start(bf16[192,1792]{1,0:T(8,128)(2,1)} %refs_4_.2), channel_id=1, source_target_pairs={{0,8},{2,10},{4,12},{6,14},{8,0},{10,2},{12,4},{14,6},{16,24},{18,... | collective-permute-start | bytes 2064392 | tf_op jit(solution)/shard_map/ppermute | solution.py:483
  25.3 1.1 copy-start.3
  26.4 1.1 copy-start.9
  27.5 7.8 %copy-start.12 = (bf16[192,1792]{1,0:T(8,128)(2,1)S(1)}, bf16[192,1792]{1,0:T(8,128)(2,1)}, u32[]{:S(2)}) copy-start(bf16[192,1792]{1,0:T(8,128)(2,1)} %copy-done.11) | copy-start | bytes 2064388
  35.3 10.2 %copy-start.4 = (bf16[192,1792]{1,0:T(8,128)(2,1)S(1)}, bf16[192,1792]{1,0:T(8,128)(2,1)}, u32[]{:S(2)}) copy-start(bf16[192,1792]{1,0:T(8,128)(2,1)} %refs_4_.2) | copy-start | bytes 2064388
  42.9 1.1 copy-start.5
  44.1 1.1 copy-start.7
  45.2 16.5 %collective-permute-start.3 = (bf16[2,2,2,1,192,128]{5,4,2,1,3,0:T(8,128)(2,1)}, bf16[2,2,2,1,192,128]{5,4,2,1,3,0:T(8,128)(2,1)}, u32[]{:S(2)}, u32[]{:S(2)}) collective-permute-start(bf16[2,2,2,1,192,128]{5,4,2,1,3,0:T(8,128)(2,1)} %bitcast.5), channel_id=1, source_target_pairs={{0,1},{1,0},{2,3},{3,2},{4,5},{5,4},{6,7},{7,6},{8,9},{9,8},{10,11... | collective-permute-start | bytes 1179656 | tf_op jit(solution)/shard_map/ppermute | solution.py:479
  45.5 43.7 %collective-permute-start.20 = (bf16[192,1792]{1,0:T(8,128)(2,1)S(1)}, bf16[192,1792]{1,0:T(8,128)(2,1)}, u32[]{:S(2)}, u32[]{:S(2)}) collective-permute-start(bf16[192,1792]{1,0:T(8,128)(2,1)S(1)} %copy-done.4), channel_id=1, source_target_pairs={{0,2},{2,0},{4,6},{6,4},{8,10},{10,8},{12,14},{14,12},{16,18},{18,... | collective-permute-start | bytes 2064392 | tf_op jit(solution)/shard_map/ppermute | solution.py:483
  50.3 39.5 %collective-permute-start.8 = (bf16[192,1792]{1,0:T(8,128)(2,1)}, bf16[192,1792]{1,0:T(8,128)(2,1)S(1)}, u32[]{:S(2)}, u32[]{:S(2)}) collective-permute-start(bf16[192,1792]{1,0:T(8,128)(2,1)} %copy-done.11), channel_id=1, source_target_pairs={{0,8},{2,10},{4,12},{6,14},{8,0},{10,2},{12,4},{14,6},{16,24},{18,... | collective-permute-start | bytes 2064392 | tf_op jit(solution)/shard_map/ppermute | solution.py:483
  53.9 1.4 copy-start.6
  55.4 1.4 copy-start.8
  61.7 28.7 %collective-permute-start.4 = (bf16[2,2,2,2,192,128]{5,4,3,2,1,0:T(8,128)(2,1)S(1)}, bf16[2,2,2,2,192,128]{5,4,3,2,1,0:T(8,128)(2,1)S(1)}, u32[]{:S(2)}, u32[]{:S(2)}) collective-permute-start(bf16[2,2,2,2,192,128]{5,4,3,2,1,0:T(8,128)(2,1)S(1)} %get-tuple-element.61), channel_id=1, source_target_pairs={{0,1},{1,0},{2,3},{3,2},{4,5},{5,4},{6,7},{7,6},{8,9},{9,8},{10,11... | collective-permute-start | bytes 2359304 | tf_op jit(solution)/shard_map/ppermute | solution.py:479
  63.0 26.9 %collective-permute-start.25 = (bf16[192,1792]{1,0:T(8,128)(2,1)S(1)}, bf16[192,1792]{1,0:T(8,128)(2,1)S(1)}, u32[]{:S(2)}, u32[]{:S(2)}) collective-permute-start(bf16[192,1792]{1,0:T(8,128)(2,1)S(1)} %collective-permute-done.1.other_ref.refs_4_), channel_id=1, source_target_pairs={{0,8},{2,10},{4,12},{6,14},{8,0},{10,2},{12,4},{14,6},{16,24},{18,... | collective-permute-start | bytes 2064392 | tf_op jit(solution)/shard_map/ppermute | solution.py:483
  65.0 24.2 %collective-permute-start.16 = (bf16[2,2,1,192,128]{4,3,1,2,0:T(8,128)(2,1)S(1)}, bf16[2,2,1,192,128]{4,3,1,2,0:T(8,128)(2,1)S(1)}, u32[]{:S(2)}, u32[]{:S(2)}) collective-permute-start(bf16[2,2,1,192,128]{4,3,1,2,0:T(8,128)(2,1)S(1)} %get-tuple-element.94), channel_id=1, source_target_pairs={{0,8},{2,10},{4,12},{6,14},{8,0},{10,2},{12,4},{14,6},{16,24},{18,... | collective-permute-start | bytes 589832 | tf_op jit(solution)/shard_map/ppermute | solution.py:483
  71.0 20.6 %copy-start.13 = (bf16[192,1792]{1,0:T(8,128)(2,1)S(1)}, bf16[192,1792]{1,0:T(8,128)(2,1)}, u32[]{:S(2)}) copy-start(bf16[192,1792]{1,0:T(8,128)(2,1)} %copy-done.11) | copy-start | bytes 2064388
  89.2 2.4 %collective-permute-start.21 = (bf16[192,1792]{1,0:T(8,128)(2,1)}, bf16[192,1792]{1,0:T(8,128)(2,1)S(1)}, u32[]{:S(2)}, u32[]{:S(2)}) collective-permute-start(bf16[192,1792]{1,0:T(8,128)(2,1)} %collective-permute-done.19.refs_5_), channel_id=1, source_target_pairs={{0,2},{2,0},{4,6},{6,4},{8,10},{10,8},{12,14},{14,12},{16,18},{18,... | collective-permute-start | bytes 2064392 | tf_op jit(solution)/shard_map/ppermute | solution.py:483
  89.3 14.0 %collective-permute-start.26 = (bf16[192,1792]{1,0:T(8,128)(2,1)S(1)}, bf16[192,1792]{1,0:T(8,128)(2,1)S(1)}, u32[]{:S(2)}, u32[]{:S(2)}) collective-permute-start(bf16[192,1792]{1,0:T(8,128)(2,1)S(1)} %collective-permute-done.1.other_ref.refs_4_), channel_id=1, source_target_pairs={{0,2},{2,0},{4,6},{6,4},{8,10},{10,8},{12,14},{14,12},{16,18},{18,... | collective-permute-start | bytes 2064392 | tf_op jit(solution)/shard_map/ppermute | solution.py:483
  89.8 2.9 %collective-permute-start.17 = (bf16[2,1,192,128]{3,2,0,1:T(8,128)(2,1)S(1)}, bf16[2,1,192,128]{3,2,0,1:T(8,128)(2,1)S(1)}, u32[]{:S(2)}, u32[]{:S(2)}) collective-permute-start(bf16[2,1,192,128]{3,2,0,1:T(8,128)(2,1)S(1)} %slice_bitcast_fusion.3), channel_id=1, source_target_pairs={{0,2},{2,0},{4,6},{6,4},{8,10},{10,8},{12,14},{14,12},{16,18},{18,... | collective-permute-start | bytes 294920 | tf_op jit(solution)/shard_map/ppermute | solution.py:483
  89.9 2.9 %collective-permute-start.18 = (bf16[2,1,192,128]{3,2,1,0:T(8,128)(2,1)S(1)}, bf16[2,1,192,128]{3,2,1,0:T(8,128)(2,1)S(1)}, u32[]{:S(2)}, u32[]{:S(2)}) collective-permute-start(bf16[2,1,192,128]{3,2,1,0:T(8,128)(2,1)S(1)} %slice_bitcast_fusion.2), channel_id=1, source_target_pairs={{0,2},{2,0},{4,6},{6,4},{8,10},{10,8},{12,14},{14,12},{16,18},{18,... | collective-permute-start | bytes 294920 | tf_op jit(solution)/shard_map/ppermute | solution.py:483
  90.3 13.0 %collective-permute-start.27 = (bf16[192,1792]{1,0:T(8,128)(2,1)S(1)}, bf16[192,1792]{1,0:T(8,128)(2,1)S(1)}, u32[]{:S(2)}, u32[]{:S(2)}) collective-permute-start(bf16[192,1792]{1,0:T(8,128)(2,1)S(1)} %collective-permute-done.25.refs_5_), channel_id=1, source_target_pairs={{0,2},{2,0},{4,6},{6,4},{8,10},{10,8},{12,14},{14,12},{16,18},{18,... | collective-permute-start | bytes 2064392 | tf_op jit(solution)/shard_map/ppermute | solution.py:483
  91.6 14.2 %collective-permute-start.9 = (bf16[192,1792]{1,0:T(8,128)(2,1)S(1)}, bf16[192,1792]{1,0:T(8,128)(2,1)S(1)}, u32[]{:S(2)}, u32[]{:S(2)}) collective-permute-start(bf16[192,1792]{1,0:T(8,128)(2,1)S(1)} %copy-done.13), channel_id=1, source_target_pairs={{0,2},{2,0},{4,6},{6,4},{8,10},{10,8},{12,14},{14,12},{16,18},{18,... | collective-permute-start | bytes 2064392 | tf_op jit(solution)/shard_map/ppermute | solution.py:483
  92.7 13.2 %collective-permute-start.10 = (bf16[192,1792]{1,0:T(8,128)(2,1)S(1)}, bf16[192,1792]{1,0:T(8,128)(2,1)S(1)}, u32[]{:S(2)}, u32[]{:S(2)}) collective-permute-start(bf16[192,1792]{1,0:T(8,128)(2,1)S(1)} %collective-permute-done.8.refs_5_), channel_id=1, source_target_pairs={{0,2},{2,0},{4,6},{6,4},{8,10},{10,8},{12,14},{14,12},{16,18},{18,... | collective-permute-start | bytes 2064392 | tf_op jit(solution)/shard_map/ppermute | solution.py:483
  92.8 12.8 %collective-permute-start.5 = (bf16[2,2,2,192,128]{4,3,2,1,0:T(8,128)(2,1)S(1)}, bf16[2,2,2,192,128]{4,3,2,1,0:T(8,128)(2,1)S(1)}, u32[]{:S(2)}, u32[]{:S(2)}) collective-permute-start(bf16[2,2,2,192,128]{4,3,2,1,0:T(8,128)(2,1)S(1)} %get-tuple-element.92), channel_id=1, source_target_pairs={{0,8},{2,10},{4,12},{6,14},{8,0},{10,2},{12,4},{14,6},{16,24},{18,... | collective-permute-start | bytes 1179656 | tf_op jit(solution)/shard_map/ppermute | solution.py:483
  100.5 2.8 %copy-start.10 = (bf16[192,1792]{1,0:T(8,128)(2,1)S(1)}, bf16[192,1792]{1,0:T(8,128)(2,1)}, u32[]{:S(2)}) copy-start(bf16[192,1792]{1,0:T(8,128)(2,1)} %refs_4_.3) | copy-start | bytes 2064388
  103.3 17.9 %collective-permute-start.32 = (bf16[192,1792]{1,0:T(8,128)(2,1)S(1)}, bf16[192,1792]{1,0:T(8,128)(2,1)S(1)}, u32[]{:S(2)}, u32[]{:S(2)}) collective-permute-start(bf16[192,1792]{1,0:T(8,128)(2,1)S(1)} %copy-done.10), channel_id=1, source_target_pairs={{0,2},{2,0},{4,6},{6,4},{8,10},{10,8},{12,14},{14,12},{16,18},{18,... | collective-permute-start | bytes 2064392 | tf_op jit(solution)/shard_map/ppermute | solution.py:483
  103.4 19.5 %collective-permute-start.33 = (bf16[192,1792]{1,0:T(8,128)(2,1)}, bf16[192,1792]{1,0:T(8,128)(2,1)S(1)}, u32[]{:S(2)}, u32[]{:S(2)}) collective-permute-start(bf16[192,1792]{1,0:T(8,128)(2,1)} %collective-permute-done.31.refs_5_), channel_id=1, source_target_pairs={{0,2},{2,0},{4,6},{6,4},{8,10},{10,8},{12,14},{14,12},{16,18},{18,... | collective-permute-start | bytes 2064392 | tf_op jit(solution)/shard_map/ppermute | solution.py:483
  105.6 8.5 %collective-permute-start.23 = (bf16[64,1792]{1,0:T(8,128)(2,1)S(1)}, bf16[64,1792]{1,0:T(8,128)(2,1)S(1)}, u32[]{:S(2)}, u32[]{:S(2)}) collective-permute-start(bf16[64,1792]{1,0:T(8,128)(2,1)S(1)} %get-tuple-element.74), channel_id=1, source_target_pairs={{0,4},{2,6},{4,0},{6,2},{8,12},{10,14},{12,8},{14,10},{16,20},{18,... | collective-permute-start | bytes 688136 | tf_op jit(solution)/shard_map/ppermute | solution.py:483
  105.8 8.5 %collective-permute-start.6 = (bf16[2,2,192,128]{3,2,1,0:T(8,128)(2,1)S(1)}, bf16[2,2,192,128]{3,2,1,0:T(8,128)(2,1)S(1)}, u32[]{:S(2)}, u32[]{:S(2)}) collective-permute-start(bf16[2,2,192,128]{3,2,1,0:T(8,128)(2,1)S(1)} %slice_bitcast_fusion.1), channel_id=1, source_target_pairs={{0,2},{2,0},{4,6},{6,4},{8,10},{10,8},{12,14},{14,12},{16,18},{18,... | collective-permute-start | bytes 589832 | tf_op jit(solution)/shard_map/ppermute | solution.py:483
  105.9 13.1 %collective-permute-start.29 = (bf16[64,1792]{1,0:T(8,128)(2,1)S(1)}, bf16[64,1792]{1,0:T(8,128)(2,1)S(1)}, u32[]{:S(2)}, u32[]{:S(2)}) collective-permute-start(bf16[64,1792]{1,0:T(8,128)(2,1)S(1)} %get-tuple-element.78), channel_id=1, source_target_pairs={{0,4},{2,6},{4,0},{6,2},{8,12},{10,14},{12,8},{14,10},{16,20},{18,... | collective-permute-start | bytes 688136 | tf_op jit(solution)/shard_map/ppermute | solution.py:483
  114.2 2.0 collective-permute-start.7
  114.3 31.9 %collective-permute-start.2 = (bf16[192,1792]{1,0:T(8,128)(2,1)S(1)}, bf16[192,1792]{1,0:T(8,128)(2,1)S(1)}, u32[]{:S(2)}, u32[]{:S(2)}) collective-permute-start(bf16[192,1792]{1,0:T(8,128)(2,1)S(1)} %input_other.1), channel_id=1, source_target_pairs={{0,1},{1,0},{2,3},{3,2},{4,5},{5,4},{6,7},{7,6},{8,9},{9,8},{10,11... | collective-permute-start | bytes 2064392 | tf_op jit(solution)/shard_map/ppermute | solution.py:479
  116.2 37.5 %collective-permute-start.22 = (bf16[64,1792]{1,0:T(8,128)(2,1)S(1)}, bf16[64,1792]{1,0:T(8,128)(2,1)S(1)}, u32[]{:S(2)}, u32[]{:S(2)}) collective-permute-start(bf16[64,1792]{1,0:T(8,128)(2,1)S(1)} %get-tuple-element.72), channel_id=1, source_target_pairs={{0,4},{2,6},{4,0},{6,2},{8,12},{10,14},{12,8},{14,10},{16,20},{18,... | collective-permute-start | bytes 688136 | tf_op jit(solution)/shard_map/ppermute | solution.py:483
  119.0 10.5 %collective-permute-start.12 = (bf16[64,1792]{1,0:T(8,128)(2,1)S(1)}, bf16[64,1792]{1,0:T(8,128)(2,1)S(1)}, u32[]{:S(2)}, u32[]{:S(2)}) collective-permute-start(bf16[64,1792]{1,0:T(8,128)(2,1)S(1)} %get-tuple-element.65), channel_id=1, source_target_pairs={{0,4},{2,6},{4,0},{6,2},{8,12},{10,14},{12,8},{14,10},{16,20},{18,... | collective-permute-start | bytes 688136 | tf_op jit(solution)/shard_map/ppermute | solution.py:483
  121.2 33.9 %collective-permute-start.24 = (bf16[64,1792]{1,0:T(8,128)(2,1)S(1)}, bf16[64,1792]{1,0:T(8,128)(2,1)S(1)}, u32[]{:S(2)}, u32[]{:S(2)}) collective-permute-start(bf16[64,1792]{1,0:T(8,128)(2,1)S(1)} %add_convert_fusion.4), channel_id=1, source_target_pairs={{0,16},{2,18},{4,20},{6,22},{8,24},{10,26},{12,28},{14,30},{16,0},... | collective-permute-start | bytes 688136 | tf_op jit(solution)/shard_map/ppermute | solution.py:483
  122.9 32.9 %collective-permute-start.28 = (bf16[64,1792]{1,0:T(8,128)(2,1)S(1)}, bf16[64,1792]{1,0:T(8,128)(2,1)S(1)}, u32[]{:S(2)}, u32[]{:S(2)}) collective-permute-start(bf16[64,1792]{1,0:T(8,128)(2,1)S(1)} %get-tuple-element.76), channel_id=1, source_target_pairs={{0,4},{2,6},{4,0},{6,2},{8,12},{10,14},{12,8},{14,10},{16,20},{18,... | collective-permute-start | bytes 688136 | tf_op jit(solution)/shard_map/ppermute | solution.py:483
  124.8 72.6 %copy-start.2 = (f32[3,64,3584]{2,1,0:T(8,128)S(1)}, f32[3,64,3584]{2,1,0:T(8,128)}, u32[]{:S(2)}) copy-start(f32[3,64,3584]{2,1,0:T(8,128)} %refs_8_.1) | copy-start | bytes 8257540
  129.6 9.1 %collective-permute-start.14 = (bf16[64,1792]{1,0:T(8,128)(2,1)S(1)}, bf16[64,1792]{1,0:T(8,128)(2,1)S(1)}, u32[]{:S(2)}, u32[]{:S(2)}) collective-permute-start(bf16[64,1792]{1,0:T(8,128)(2,1)S(1)} %get-tuple-element.68), channel_id=1, source_target_pairs={{0,4},{2,6},{4,0},{6,2},{8,12},{10,14},{12,8},{14,10},{16,20},{18,... | collective-permute-start | bytes 688136 | tf_op jit(solution)/shard_map/ppermute | solution.py:483
  129.6 67.8 %copy-start = (f32[3,64,3584]{2,1,0:T(8,128)S(1)}, f32[3,64,3584]{2,1,0:T(8,128)}, u32[]{:S(2)}) copy-start(f32[3,64,3584]{2,1,0:T(8,128)} %refs_6_.1) | copy-start | bytes 8257540
  129.6 67.8 %copy-start.1 = (f32[3,64,3584]{2,1,0:T(8,128)S(1)}, f32[3,64,3584]{2,1,0:T(8,128)}, u32[]{:S(2)}) copy-start(f32[3,64,3584]{2,1,0:T(8,128)} %refs_7_.1) | copy-start | bytes 8257540
  138.7 6.9 %collective-permute-start.35 = (bf16[64,1792]{1,0:T(8,128)(2,1)S(1)}, bf16[64,1792]{1,0:T(8,128)(2,1)S(1)}, u32[]{:S(2)}, u32[]{:S(2)}) collective-permute-start(bf16[64,1792]{1,0:T(8,128)(2,1)S(1)} %get-tuple-element.82), channel_id=1, source_target_pairs={{0,4},{2,6},{4,0},{6,2},{8,12},{10,14},{12,8},{14,10},{16,20},{18,... | collective-permute-start | bytes 688136 | tf_op jit(solution)/shard_map/ppermute | solution.py:483
  145.6 6.0 %collective-permute-start.37 = (bf16[64,1792]{1,0:T(8,128)(2,1)S(1)}, bf16[64,1792]{1,0:T(8,128)(2,1)S(1)}, u32[]{:S(2)}, u32[]{:S(2)}) collective-permute-start(bf16[64,1792]{1,0:T(8,128)(2,1)S(1)} %get-tuple-element.85), channel_id=1, source_target_pairs={{0,4},{2,6},{4,0},{6,2},{8,12},{10,14},{12,8},{14,10},{16,20},{18,... | collective-permute-start | bytes 688136 | tf_op jit(solution)/shard_map/ppermute | solution.py:483
  146.2 22.5 %collective-permute-start.30 = (bf16[64,1792]{1,0:T(8,128)(2,1)S(1)}, bf16[64,1792]{1,0:T(8,128)(2,1)S(1)}, u32[]{:S(2)}, u32[]{:S(2)}) collective-permute-start(bf16[64,1792]{1,0:T(8,128)(2,1)S(1)} %add_convert_fusion.3), channel_id=1, source_target_pairs={{0,16},{2,18},{4,20},{6,22},{8,24},{10,26},{12,28},{14,30},{16,0},... | collective-permute-start | bytes 688136 | tf_op jit(solution)/shard_map/ppermute | solution.py:483
  151.6 26.9 %collective-permute-start.36 = (bf16[64,1792]{1,0:T(8,128)(2,1)S(1)}, bf16[64,1792]{1,0:T(8,128)(2,1)S(1)}, u32[]{:S(2)}, u32[]{:S(2)}) collective-permute-start(bf16[64,1792]{1,0:T(8,128)(2,1)S(1)} %add_convert_fusion.2), channel_id=1, source_target_pairs={{0,16},{2,18},{4,20},{6,22},{8,24},{10,26},{12,28},{14,30},{16,0},... | collective-permute-start | bytes 688136 | tf_op jit(solution)/shard_map/ppermute | solution.py:483
  153.7 47.8 %collective-permute-start.11 = (bf16[128,1792]{1,0:T(8,128)(2,1)S(1)}, bf16[128,1792]{1,0:T(8,128)(2,1)S(1)}, u32[]{:S(2)}, u32[]{:S(2)}) collective-permute-start(bf16[128,1792]{1,0:T(8,128)(2,1)S(1)} %get-tuple-element.63), channel_id=1, source_target_pairs={{0,4},{2,6},{4,0},{6,2},{8,12},{10,14},{12,8},{14,10},{16,20},{18,... | collective-permute-start | bytes 1376264 | tf_op jit(solution)/shard_map/ppermute | solution.py:483
  155.1 42.3 %collective-permute-start.34 = (bf16[128,1792]{1,0:T(8,128)(2,1)S(1)}, bf16[128,1792]{1,0:T(8,128)(2,1)S(1)}, u32[]{:S(2)}, u32[]{:S(2)}) collective-permute-start(bf16[128,1792]{1,0:T(8,128)(2,1)S(1)} %get-tuple-element.80), channel_id=1, source_target_pairs={{0,4},{2,6},{4,0},{6,2},{8,12},{10,14},{12,8},{14,10},{16,20},{18,... | collective-permute-start | bytes 1376264 | tf_op jit(solution)/shard_map/ppermute | solution.py:483
  155.8 45.7 %collective-permute-start.13 = (bf16[64,1792]{1,0:T(8,128)(2,1)S(1)}, bf16[64,1792]{1,0:T(8,128)(2,1)S(1)}, u32[]{:S(2)}, u32[]{:S(2)}) collective-permute-start(bf16[64,1792]{1,0:T(8,128)(2,1)S(1)} %add_convert_fusion.6), channel_id=1, source_target_pairs={{0,16},{2,18},{4,20},{6,22},{8,24},{10,26},{12,28},{14,30},{16,0},... | collective-permute-start | bytes 688136 | tf_op jit(solution)/shard_map/ppermute | solution.py:483
  168.7 32.8 %collective-permute-start.15 = (bf16[64,1792]{1,0:T(8,128)(2,1)S(1)}, bf16[64,1792]{1,0:T(8,128)(2,1)S(1)}, u32[]{:S(2)}, u32[]{:S(2)}) collective-permute-start(bf16[64,1792]{1,0:T(8,128)(2,1)S(1)} %add_convert_fusion.5), channel_id=1, source_target_pairs={{0,16},{2,18},{4,20},{6,22},{8,24},{10,26},{12,28},{14,30},{16,0},... | collective-permute-start | bytes 688136 | tf_op jit(solution)/shard_map/ppermute | solution.py:483
  178.5 18.9 %collective-permute-start.38 = (bf16[64,1792]{1,0:T(8,128)(2,1)S(1)}, bf16[64,1792]{1,0:T(8,128)(2,1)S(1)}, u32[]{:S(2)}, u32[]{:S(2)}) collective-permute-start(bf16[64,1792]{1,0:T(8,128)(2,1)S(1)} %add_convert_fusion.1), channel_id=1, source_target_pairs={{0,16},{2,18},{4,20},{6,22},{8,24},{10,26},{12,28},{14,30},{16,0},... | collective-permute-start | bytes 688136 | tf_op jit(solution)/shard_map/ppermute | solution.py:483
